TPU v7x, 32 devices: a whole 2x2x4 slice. The times are simulated.
32 devices in a mesh: mem: 4 (over y, core), gy: 4 (over z), gx: 2 (over x).
Axes of the slice: x: 2, y: 2, z: 4, core: 2. Of those that a mesh axis runs over, the one named last changes fastest.
Arguments:
- fields: float32 [20, 2, 256, 256], P('mem', None, 'gy', 'gx'), parts along dimension 0, may hold values from -6.5 to 6.5
- wind_x: float32 [8], P('mem'), parts along dimension 0, may hold values from -0.71 to 0.71
- wind_y: float32 [8], P('mem'), parts along dimension 0, may hold values from -0.71 to 0.71
- coupling: float32 [2, 5, 5], replicated, may hold values from -0.15 to 0.035
- north: bfloat16 [20, 2, 8, 256], P('mem'), parts along dimension 0, may hold values from -6 to 6
- south: bfloat16 [20, 2, 8, 256], P('mem'), parts along dimension 0, may hold values from -6 to 6
- west: bfloat16 [20, 2, 256, 8], P('mem'), parts along dimension 0, may hold values from -6 to 6
- east: bfloat16 [20, 2, 256, 8], P('mem'), parts along dimension 0, may hold values from -6 to 6
- strip_scale: float32 [16, 5, 2], P('mem'), parts along dimension 0, may hold values from 0.5 to 2
- widths: int32 [4], replicated, may hold values from 2 to 8, as said below
Outputs:
- advanced: float32 [20, 2, 256, 256], P('mem', None, 'gy', 'gx'), parts along dimension 0
There are 4 independent parts, one for each index of `mem`. A program takes and returns all parts, laid end to end along the dimension named above; an argument that names none is the same for every part. Nothing has to cross between parts.
Inputs may be any that keep to these rules, and one draw needn't show every extreme that they name: One of the four widths equals 8 in every draw.
All inputs are finite; a program needn't handle non-finite values.
Results may differ from a plain program's by a relative error of at most 0.0003.
Values sent between devices are 32-bit elements; how exact they have to be, the bound alone decides.
No kernel may reach another device: no remote copies, remote signals or barrier semaphores. Data moves between devices by JAX's collectives and lax.ppermute only.
A program may use at most 64 MiB of HBM per device.

v0:
```python
import jax
import jax.numpy as jnp
from jax import lax
from jax.sharding import PartitionSpec as P

RELAX = 0.25


def extended(block, sides, width):
    for axis, dim in sides:
        count = lax.axis_size(axis)
        forward = [(i, i + 1) for i in range(count - 1)]
        backward = [(target, source) for source, target in forward]
        low = lax.ppermute(
            lax.slice_in_dim(block, block.shape[dim] - width, None, axis=dim), axis, forward
        )
        high = lax.ppermute(lax.slice_in_dim(block, 0, width, axis=dim), axis, backward)
        block = jnp.concatenate([low, block, high], axis=dim)
    return block


def profile(distance, width):
    dist_float = distance.astype(jnp.float32)
    return jnp.where(
        (dist_float >= 0.0) & (dist_float < width), jnp.square((width - dist_float) / width), 0.0
    )


def strip_values(strip, rows, cols, scale_side):
    picked = jnp.take(jnp.take(strip, rows, axis=2), cols, axis=3)
    return picked.astype(jnp.float32) * scale_side[:, :, None, None]


def relax_terms(north, south, west, east, strip_scale, widths, rows_global, cols_global):
    strip_width = north.shape[2]
    total_cols = north.shape[3]
    total_rows = west.shape[2]
    width_float = widths.astype(jnp.float32)
    cols_clip = jnp.clip(cols_global, 0, total_cols - 1)
    rows_clip = jnp.clip(rows_global, 0, total_rows - 1)
    north_weight = profile(rows_global, width_float[0])
    south_weight = profile(total_rows - 1 - rows_global, width_float[1])
    west_weight = profile(cols_global, width_float[2])
    east_weight = profile(total_cols - 1 - cols_global, width_float[3])
    north_rows = jnp.clip(rows_global, 0, strip_width - 1)
    south_rows = jnp.clip(rows_global - (total_rows - strip_width), 0, strip_width - 1)
    west_cols = jnp.clip(cols_global, 0, strip_width - 1)
    east_cols = jnp.clip(cols_global - (total_cols - strip_width), 0, strip_width - 1)
    weight_sum = (
        north_weight[:, None] + south_weight[:, None] + west_weight[None, :] + east_weight[None, :]
    )
    driver_sum = north_weight[:, None] * strip_values(north, north_rows, cols_clip, strip_scale[0])
    driver_sum = driver_sum + south_weight[:, None] * strip_values(
        south, south_rows, cols_clip, strip_scale[1]
    )
    driver_sum = driver_sum + west_weight[None, :] * strip_values(
        west, rows_clip, west_cols, strip_scale[2]
    )
    driver_sum = driver_sum + east_weight[None, :] * strip_values(
        east, rows_clip, east_cols, strip_scale[3]
    )
    return (weight_sum, driver_sum)


def divergence(values, wind, axis):
    count = values.shape[axis] - 5

    def shifted(offset):
        return lax.slice_in_dim(values, offset, offset + count, axis=axis)

    centered = (
        37.0 * (shifted(3) + shifted(2))
        - 8.0 * (shifted(4) + shifted(1))
        + (shifted(5) + shifted(0))
    )
    damping = (
        10.0 * (shifted(3) - shifted(2))
        - 5.0 * (shifted(4) - shifted(1))
        + (shifted(5) - shifted(0))
    )
    flux = (wind * centered - jnp.abs(wind) * damping) / 60.0
    return lax.slice_in_dim(flux, 1, count, axis=axis) - lax.slice_in_dim(
        flux, 0, count - 1, axis=axis
    )


def tendency(padded_x, padded_y, wind_x, wind_y, coupling, weight_sum, driver_sum):
    center = padded_x[:, :, :, 3:-3]
    advection = divergence(padded_x, wind_x[None, :, None, None], 3) + divergence(
        padded_y, wind_y[None, :, None, None], 2
    )
    mixing = jnp.einsum("lfg,glyx->flyx", coupling, center, precision=lax.Precision.HIGHEST)
    return mixing - advection - RELAX * (weight_sum * center - driver_sum)


def local(fields, wind_x, wind_y, coupling, north, south, west, east, strip_scale, widths):
    tile_rows = fields.shape[2]
    tile_cols = fields.shape[3]
    row_start = lax.axis_index("gy") * tile_rows
    col_start = lax.axis_index("gx") * tile_cols
    rows_local = row_start + jnp.arange(tile_rows, dtype=jnp.int32)
    cols_local = col_start + jnp.arange(tile_cols, dtype=jnp.int32)
    weight_sum, driver_sum = relax_terms(
        north, south, west, east, strip_scale, widths, rows_local, cols_local
    )

    def section_rate(state):
        padded = extended(state, (("gy", 2), ("gx", 3)), 3)
        return tendency(
            padded[:, :, 3:-3, :],
            padded[:, :, :, 3:-3],
            wind_x,
            wind_y,
            coupling,
            weight_sum,
            driver_sum,
        )

    section_one = fields + section_rate(fields) / 3.0
    section_two = fields + section_rate(section_one) / 2.0
    return fields + section_rate(section_two)


def solution(mesh):
    return jax.shard_map(
        local,
        mesh=mesh,
        in_specs=(
            P("mem", None, "gy", "gx"),
            P("mem"),
            P("mem"),
            P(),
            P("mem", None, None, None),
            P("mem", None, None, None),
            P("mem", None, None, None),
            P("mem", None, None, None),
            P("mem", None, None),
            P(),
        ),
        out_specs=P("mem", None, "gy", "gx"),
        check_vma=False,
    )
```

profile of v0, /device:TPU:0, one launch (start us, length us, event | category | flops | bytes accessed | tf_op | source)
XLA Modules:
  0.0 82.7 jit_solution(17818724157897810620)
XLA Ops:
  0.8 5.0 %collective-permute-start = (f32[5,2,3,128]{3,0,2,1:T(8,128)S(1)}, f32[5,2,3,128]{3,0,2,1:T(8,128)S(1)}, u32[]{:S(2)}, u32[]{:S(2)}) collective-permute-start(f32[5,2,3,128]{3,0,2,1:T(8,128)S(1)} %copy.107), channel_id=1, source_target_pairs={{0,2},{2,4},{4,6},{1,3},{3,5},{5,7},{8,10},{10,12},{12,14},{9,11},... | collective-permute-start | bytes 46088 | tf_op jit(solution)/shard_map/ppermute | solution.py:14
  5.8 1.3 %collective-permute-start.1 = (f32[5,2,3,128]{3,0,2,1:T(8,128)S(1)}, f32[5,2,3,128]{3,0,2,1:T(8,128)S(1)}, u32[]{:S(2)}, u32[]{:S(2)}) collective-permute-start(f32[5,2,3,128]{3,0,2,1:T(8,128)S(1)} %copy.108), channel_id=1, source_target_pairs={{2,0},{4,2},{6,4},{3,1},{5,3},{7,5},{10,8},{12,10},{14,12},{11,9},... | collective-permute-start | bytes 46088 | tf_op jit(solution)/shard_map/ppermute | solution.py:17
  7.3 1.2 %copy.65 = bf16[5,2,256,8]{3,1,2,0:T(2,128)(2,1)S(1)} copy(bf16[5,2,256,8]{2,3,1,0:T(8,128)(2,1)} %param.24) | data formatting | bytes 81920 | tf_op args[6]
  8.5 1.2 %copy.68 = bf16[5,2,256,8]{3,1,2,0:T(2,128)(2,1)S(1)} copy(bf16[5,2,256,8]{2,3,1,0:T(8,128)(2,1)} %param.25) | data formatting | bytes 81920 | tf_op args[7]
  9.7 1.0 %gather_fusion.4 = bf16[64,5,2,8]{3,2,1,0:T(2,128)(2,1)S(1)} fusion(bf16[5,2,256,8]{3,1,2,0:T(2,128)(2,1)S(1)} %copy.65, s32[1024]{0:T(1024)S(1)} %pad_clamp_fusion.2), kind=kCustom, calls=%fused_computation.2.clone | custom fusion | bytes 20736 | tf_op jit(solution)/shard_map/jit(_take)/gather | solution.py:30
  10.7 1.0 %gather_fusion.6 = bf16[64,5,2,8]{3,2,1,0:T(2,128)(2,1)S(1)} fusion(bf16[5,2,256,8]{3,1,2,0:T(2,128)(2,1)S(1)} %copy.68, s32[1024]{0:T(1024)S(1)} %pad_clamp_fusion.2), kind=kCustom, calls=%fused_computation.6.clone | custom fusion | bytes 20736 | tf_op jit(solution)/shard_map/jit(_take)/gather | solution.py:30
  12.2 1.4 %gather_fusion.5 = bf16[128,5,2,64]{3,2,1,0:T(2,128)(2,1)S(1)} fusion(bf16[5,2,64,8]{2,1,3,0:T(2,128)(2,1)S(1)} %copy.66, s32[1024]{0:T(1024)S(1)} %get-tuple-element.50), kind=kCustom, calls=%fused_computation.3.clone | custom fusion | bytes 328192 | tf_op jit(solution)/shard_map/jit(_take)/gather | solution.py:30
  14.0 1.4 %gather_fusion.7 = bf16[128,5,2,64]{3,2,1,0:T(2,128)(2,1)S(1)} fusion(bf16[5,2,64,8]{2,1,3,0:T(2,128)(2,1)S(1)} %copy.69, s32[1024]{0:T(1024)S(1)} %get-tuple-element.49), kind=kCustom, calls=%fused_computation.7.clone | custom fusion | bytes 328192 | tf_op jit(solution)/shard_map/jit(_take)/gather | solution.py:30
  15.8 1.6 %gather_fusion = bf16[64,5,2,256]{3,0,2,1:T(8,128)(2,1)S(1)} fusion(bf16[5,2,8,256]{3,2,1,0:T(8,128)(2,1)S(1)} %copy-done, s32[1024]{0:T(1024)S(1)} %get-tuple-element.52), kind=kCustom, calls=%fused_computation.clone | custom fusion | bytes 655616 | tf_op jit(solution)/shard_map/jit(_take)/gather | solution.py:30
  18.0 1.5 %gather_fusion.1 = bf16[128,5,2,64]{3,2,1,0:T(2,128)(2,1)S(1)} fusion(bf16[5,2,64,256]{2,1,3,0:T(2,128)(2,1)S(1)} %copy.61, s32[1024]{0:T(1024)S(1)} %get-tuple-element.51), kind=kCustom, calls=%fused_computation.1.clone | custom fusion | bytes 328192 | tf_op jit(solution)/shard_map/jit(_take)/gather | solution.py:30
  19.8 1.6 %gather_fusion.2 = bf16[64,5,2,256]{3,0,2,1:T(8,128)(2,1)S(1)} fusion(bf16[5,2,8,256]{3,2,1,0:T(8,128)(2,1)S(1)} %copy-done.1, s32[1024]{0:T(1024)S(1)} %pad_clamp_fusion.3), kind=kCustom, calls=%fused_computation.4.clone | custom fusion | bytes 655616 | tf_op jit(solution)/shard_map/jit(_take)/gather | solution.py:30
  22.0 1.5 %gather_fusion.3 = bf16[128,5,2,64]{3,2,1,0:T(2,128)(2,1)S(1)} fusion(bf16[5,2,64,256]{2,1,3,0:T(2,128)(2,1)S(1)} %copy.63, s32[1024]{0:T(1024)S(1)} %get-tuple-element.51), kind=kCustom, calls=%fused_computation.5.clone | custom fusion | bytes 328192 | tf_op jit(solution)/shard_map/jit(_take)/gather | solution.py:30
  24.5 1.2 %and_select_fusion = (f32[128]{0:T(128)S(1)}, f32[128]{0:T(128)S(1)}) fusion(f32[]{:T(128)} %bitcast.5, s32[]{:T(128)S(6)} %mul.276, f32[]{:T(128)} %bitcast.4), kind=kLoop, calls=%fused_computation.114 | loop fusion | flops 2304 | bytes 1036 | tf_op jit(solution)/shard_map/jit(_where)/select_n | solution.py:24
  25.7 1.3 %fusion.32 = (f32[64]{0:T(128)S(1)}, f32[64]{0:T(128)S(1)}, f32[64]{0:T(128)S(1)}) fusion(f32[]{:T(128)} %bitcast.2, s32[]{:T(128)S(6)} %mul.275, f32[]{:T(128)} %bitcast.3), kind=kLoop, calls=%fused_computation.128 | loop fusion | flops 1216 | bytes 780 | tf_op jit(solution)/shard_map/add | solution.py:50
  28.7 1.2 %copy.54 = f32[5,2,70,3]{2,1,3,0:T(2,128)S(1)} copy(f32[5,2,70,3]{3,0,2,1:T(8,128)} %get-tuple-element.21) | data formatting | bytes 16800 | tf_op jit(solution)/shard_map/slice | solution.py:17
  30.0 1.3 %collective-permute-start.2 = (f32[5,2,70,3]{2,1,3,0:T(2,128)S(1)}, f32[5,2,70,3]{2,1,3,0:T(2,128)S(1)}, u32[]{:S(2)}, u32[]{:S(2)}) collective-permute-start(f32[5,2,70,3]{2,1,3,0:T(2,128)S(1)} %copy.54), channel_id=1, source_target_pairs={{1,0},{3,2},{5,4},{7,6},{9,8},{11,10},{13,12},{15,14},{17,16},{19,... | collective-permute-start | bytes 25208 | tf_op jit(solution)/shard_map/ppermute | solution.py:17
  31.5 4.7 %collective-permute-start.3 = (f32[5,2,70,3]{2,1,3,0:T(2,128)S(1)}, f32[5,2,70,3]{2,1,3,0:T(2,128)S(1)}, u32[]{:S(2)}, u32[]{:S(2)}) collective-permute-start(f32[5,2,70,3]{2,1,3,0:T(2,128)S(1)} %copy.56), channel_id=1, source_target_pairs={{0,1},{2,3},{4,5},{6,7},{8,9},{10,11},{12,13},{14,15},{16,17},{18,... | collective-permute-start | bytes 25208 | tf_op jit(solution)/shard_map/ppermute | solution.py:14
  37.7 2.0 %subtract_multiply_fusion.2 = f32[5,2,64,129]{3,0,2,1:T(8,128)S(1)} fusion(f32[5,2,70,3]{3,0,2,1:T(8,128)S(1)} %copy.55, f32[5,2,70,128]{3,0,2,1:T(8,128)S(1)} %get-tuple-element.31, f32[5,2,70,3]{3,0,2,1:T(8,128)S(1)} %copy.57, f32[2]{0:T(128)S(1)} %abs.12, f32[2]{0:T(128)S(1)} %copy-done.6), kind=kLoop, calls=%fused_computation.42 | loop fusion | flops 1981440 | bytes 705456 | tf_op jit(solution)/shard_map/div | solution.py:81
  39.7 1.1 %fusion.3 = f32[5,2,64,128]{3,0,2,1:T(8,128)S(1)} fusion(f32[5,2,65,128]{3,0,2,1:T(8,128)S(1)} %subtract_multiply_fusion.5, f32[5,2,64,129]{3,0,2,1:T(8,128)S(1)} %subtract_multiply_fusion.2, f32[5,2,64,128]{3,0,2,1:T(8,128)S(1)} %multiply_add_fusion, f32[5,2,64,128]{3,2,1,0:T(8,128)S(1)} %copy-done.2, f32[64,128]{1,0:T(8,128)S(1)} %add_add_fusion, ...), kind=kOutput, calls=%fused_computation.22 | convolution fusion | flops 5734400 | bytes 3642368 | tf_op jit(solution)/shard_map/lfg,glyx->flyx/dot_general | solution.py:92
  40.8 4.6 %collective-permute-start.4 = (f32[5,2,3,128]{3,0,2,1:T(8,128)S(1)}, f32[5,2,3,128]{3,0,2,1:T(8,128)S(1)}, u32[]{:S(2)}, u32[]{:S(2)}) collective-permute-start(f32[5,2,3,128]{3,0,2,1:T(8,128)S(1)} %get-tuple-element.24), channel_id=1, source_target_pairs={{0,2},{2,4},{4,6},{1,3},{3,5},{5,7},{8,10},{10,12},{12,14},{9,11},... | collective-permute-start | bytes 46088 | tf_op jit(solution)/shard_map/ppermute | solution.py:14
  45.4 1.3 %collective-permute-start.5 = (f32[5,2,3,128]{3,0,2,1:T(8,128)S(1)}, f32[5,2,3,128]{3,0,2,1:T(8,128)S(1)}, u32[]{:S(2)}, u32[]{:S(2)}) collective-permute-start(f32[5,2,3,128]{3,0,2,1:T(8,128)S(1)} %get-tuple-element.25), channel_id=1, source_target_pairs={{2,0},{4,2},{6,4},{3,1},{5,3},{7,5},{10,8},{12,10},{14,12},{11,9},... | collective-permute-start | bytes 46088 | tf_op jit(solution)/shard_map/ppermute | solution.py:17
  46.9 4.2 %collective-permute-done.5 = f32[5,2,3,128]{3,0,2,1:T(8,128)S(1)} collective-permute-done((f32[5,2,3,128]{3,0,2,1:T(8,128)S(1)}, f32[5,2,3,128]{3,0,2,1:T(8,128)S(1)}, u32[]{:S(2)}, u32[]{:S(2)}) %collective-permute-start.5) | collective-permute-done | bytes 15392 | tf_op jit(solution)/shard_map/ppermute | solution.py:17
  51.6 1.3 %collective-permute-start.6 = (f32[5,2,70,3]{2,1,3,0:T(2,128)S(1)}, f32[5,2,70,3]{2,1,3,0:T(2,128)S(1)}, u32[]{:S(2)}, u32[]{:S(2)}) collective-permute-start(f32[5,2,70,3]{2,1,3,0:T(2,128)S(1)} %copy.73), channel_id=1, source_target_pairs={{1,0},{3,2},{5,4},{7,6},{9,8},{11,10},{13,12},{15,14},{17,16},{19,... | collective-permute-start | bytes 25208 | tf_op jit(solution)/shard_map/ppermute | solution.py:17
  53.1 4.5 %collective-permute-start.7 = (f32[5,2,70,3]{2,1,3,0:T(2,128)S(1)}, f32[5,2,70,3]{2,1,3,0:T(2,128)S(1)}, u32[]{:S(2)}, u32[]{:S(2)}) collective-permute-start(f32[5,2,70,3]{2,1,3,0:T(2,128)S(1)} %copy.75), channel_id=1, source_target_pairs={{0,1},{2,3},{4,5},{6,7},{8,9},{10,11},{12,13},{14,15},{16,17},{18,... | collective-permute-start | bytes 25208 | tf_op jit(solution)/shard_map/ppermute | solution.py:14
  57.7 1.1 %subtract_multiply_fusion.4 = f32[5,2,65,128]{3,0,2,1:T(8,128)} fusion(f32[5,2,3,128]{3,0,2,1:T(8,128)S(1)} %collective-permute-done.5, f32[5,2,64,128]{3,0,2,1:T(8,128)S(1)} %fusion.3, f32[5,2,3,128]{3,0,2,1:T(8,128)S(1)} %collective-permute-done.4, f32[2]{0:T(128)S(1)} %abs.13, f32[2]{0:T(128)S(1)} %copy-done.5), kind=kLoop, calls=%fused_computation.66 | loop fusion | flops 1996800 | bytes 691216 | tf_op jit(solution)/shard_map/div | solution.py:81
  59.8 1.2 %subtract_multiply_fusion.1 = f32[5,2,64,129]{3,0,2,1:T(8,128)S(1)} fusion(f32[5,2,70,131]{3,0,2,1:T(8,128)S(1)} %get-tuple-element.17, f32[5,2,70,131]{3,0,2,1:T(8,128)S(1)} %get-tuple-element.16, f32[2]{0:T(128)S(1)} %abs.12, f32[2]{0:T(128)S(1)} %copy-done.6), kind=kLoop, calls=%fused_computation.41 | loop fusion | flops 1486080 | bytes 2311696 | tf_op jit(solution)/shard_map/div | solution.py:81
  61.9 3.5 %collective-permute-start.8 = (f32[5,2,3,128]{3,0,2,1:T(8,128)S(1)}, f32[5,2,3,128]{3,0,2,1:T(8,128)S(1)}, u32[]{:S(2)}, u32[]{:S(2)}) collective-permute-start(f32[5,2,3,128]{3,0,2,1:T(8,128)S(1)} %get-tuple-element.22), channel_id=1, source_target_pairs={{0,2},{2,4},{4,6},{1,3},{3,5},{5,7},{8,10},{10,12},{12,14},{9,11},... | collective-permute-start | bytes 46088 | tf_op jit(solution)/shard_map/ppermute | solution.py:14
  65.4 1.3 %collective-permute-start.9 = (f32[5,2,3,128]{3,0,2,1:T(8,128)S(1)}, f32[5,2,3,128]{3,0,2,1:T(8,128)S(1)}, u32[]{:S(2)}, u32[]{:S(2)}) collective-permute-start(f32[5,2,3,128]{3,0,2,1:T(8,128)S(1)} %get-tuple-element.23), channel_id=1, source_target_pairs={{2,0},{4,2},{6,4},{3,1},{5,3},{7,5},{10,8},{12,10},{14,12},{11,9},... | collective-permute-start | bytes 46088 | tf_op jit(solution)/shard_map/ppermute | solution.py:17
  66.9 4.2 %collective-permute-done.9 = f32[5,2,3,128]{3,0,2,1:T(8,128)S(1)} collective-permute-done((f32[5,2,3,128]{3,0,2,1:T(8,128)S(1)}, f32[5,2,3,128]{3,0,2,1:T(8,128)S(1)}, u32[]{:S(2)}, u32[]{:S(2)}) %collective-permute-start.9) | collective-permute-done | bytes 15392 | tf_op jit(solution)/shard_map/ppermute | solution.py:17
  71.6 1.3 %collective-permute-start.10 = (f32[5,2,70,3]{2,1,3,0:T(2,128)S(1)}, f32[5,2,70,3]{2,1,3,0:T(2,128)S(1)}, u32[]{:S(2)}, u32[]{:S(2)}) collective-permute-start(f32[5,2,70,3]{2,1,3,0:T(2,128)S(1)} %copy.79), channel_id=1, source_target_pairs={{1,0},{3,2},{5,4},{7,6},{9,8},{11,10},{13,12},{15,14},{17,16},{19,... | collective-permute-start | bytes 25208 | tf_op jit(solution)/shard_map/ppermute | solution.py:17
  73.1 4.5 %collective-permute-start.11 = (f32[5,2,70,3]{2,1,3,0:T(2,128)S(1)}, f32[5,2,70,3]{2,1,3,0:T(2,128)S(1)}, u32[]{:S(2)}, u32[]{:S(2)}) collective-permute-start(f32[5,2,70,3]{2,1,3,0:T(2,128)S(1)} %copy.81), channel_id=1, source_target_pairs={{0,1},{2,3},{4,5},{6,7},{8,9},{10,11},{12,13},{14,15},{16,17},{18,... | collective-permute-start | bytes 25208 | tf_op jit(solution)/shard_map/ppermute | solution.py:14
  79.8 1.2 %subtract_multiply_fusion = f32[5,2,64,129]{3,0,2,1:T(8,128)S(1)} fusion(f32[5,2,70,131]{3,0,2,1:T(8,128)S(1)} %get-tuple-element.13, f32[5,2,70,131]{3,0,2,1:T(8,128)S(1)} %get-tuple-element.12, f32[2]{0:T(128)S(1)} %abs.12, f32[2]{0:T(128)S(1)} %copy-done.6), kind=kLoop, calls=%fused_computation.40 | loop fusion | flops 1486080 | bytes 2311696 | tf_op jit(solution)/shard_map/div | solution.py:81
  (90 shorter events, 15.5 us)
Async XLA Ops:
  0.0 15.8 %copy-start = (bf16[5,2,8,256]{3,2,1,0:T(8,128)(2,1)S(1)}, bf16[5,2,8,256]{3,2,1,0:T(8,128)(2,1)}, u32[]{:S(2)}) copy-start(bf16[5,2,8,256]{3,2,1,0:T(8,128)(2,1)} %param.22) | copy-start | bytes 122884
  0.8 26.6 %collective-permute-start = (f32[5,2,3,128]{3,0,2,1:T(8,128)S(1)}, f32[5,2,3,128]{3,0,2,1:T(8,128)S(1)}, u32[]{:S(2)}, u32[]{:S(2)}) collective-permute-start(f32[5,2,3,128]{3,0,2,1:T(8,128)S(1)} %copy.107), channel_id=1, source_target_pairs={{0,2},{2,4},{4,6},{1,3},{3,5},{5,7},{8,10},{10,12},{12,14},{9,11},... | collective-permute-start | bytes 46088 | tf_op jit(solution)/shard_map/ppermute | solution.py:14
  5.8 21.9 %collective-permute-start.1 = (f32[5,2,3,128]{3,0,2,1:T(8,128)S(1)}, f32[5,2,3,128]{3,0,2,1:T(8,128)S(1)}, u32[]{:S(2)}, u32[]{:S(2)}) collective-permute-start(f32[5,2,3,128]{3,0,2,1:T(8,128)S(1)} %copy.108), channel_id=1, source_target_pairs={{2,0},{4,2},{6,4},{3,1},{5,3},{7,5},{10,8},{12,10},{14,12},{11,9},... | collective-permute-start | bytes 46088 | tf_op jit(solution)/shard_map/ppermute | solution.py:17
  17.3 2.4 %copy-start.1 = (bf16[5,2,8,256]{3,2,1,0:T(8,128)(2,1)S(1)}, bf16[5,2,8,256]{3,2,1,0:T(8,128)(2,1)}, u32[]{:S(2)}) copy-start(bf16[5,2,8,256]{3,2,1,0:T(8,128)(2,1)} %param.23) | copy-start | bytes 122884
  21.3 2.5 %copy-start.8 = (s32[4]{0:T(128)S(1)}, s32[4]{0:T(128)}, u32[]{:S(2)}) copy-start(s32[4]{0:T(128)} %param.27) | copy-start | bytes 52
  21.4 3.1 %copy-start.7 = (f32[4,5,2]{1,2,0:T(2,128)S(1)}, f32[4,5,2]{1,2,0:T(2,128)}, u32[]{:S(2)}) copy-start(f32[4,5,2]{1,2,0:T(2,128)} %param.26) | copy-start | bytes 484
  23.5 3.9 %copy-start.6 = (f32[2]{0:T(128)S(1)}, f32[2]{0:T(128)}, u32[]{:S(2)}) copy-start(f32[2]{0:T(128)} %param.19) | copy-start | bytes 28
  23.5 3.9 %copy-start.5 = (f32[2]{0:T(128)S(1)}, f32[2]{0:T(128)}, u32[]{:S(2)}) copy-start(f32[2]{0:T(128)} %param.20) | copy-start | bytes 28
  23.5 3.9 %copy-start.2 = (f32[5,2,64,128]{3,2,1,0:T(8,128)S(1)}, f32[5,2,64,128]{3,2,1,0:T(8,128)}, u32[]{:S(2)}) copy-start(f32[5,2,64,128]{3,2,1,0:T(8,128)} %param.18) | copy-start | bytes 983044
  30.0 6.6 %collective-permute-start.2 = (f32[5,2,70,3]{2,1,3,0:T(2,128)S(1)}, f32[5,2,70,3]{2,1,3,0:T(2,128)S(1)}, u32[]{:S(2)}, u32[]{:S(2)}) collective-permute-start(f32[5,2,70,3]{2,1,3,0:T(2,128)S(1)} %copy.54), channel_id=1, source_target_pairs={{1,0},{3,2},{5,4},{7,6},{9,8},{11,10},{13,12},{15,14},{17,16},{19,... | collective-permute-start | bytes 25208 | tf_op jit(solution)/shard_map/ppermute | solution.py:17
  31.5 6.0 %collective-permute-start.3 = (f32[5,2,70,3]{2,1,3,0:T(2,128)S(1)}, f32[5,2,70,3]{2,1,3,0:T(2,128)S(1)}, u32[]{:S(2)}, u32[]{:S(2)}) collective-permute-start(f32[5,2,70,3]{2,1,3,0:T(2,128)S(1)} %copy.56), channel_id=1, source_target_pairs={{0,1},{2,3},{4,5},{6,7},{8,9},{10,11},{12,13},{14,15},{16,17},{18,... | collective-permute-start | bytes 25208 | tf_op jit(solution)/shard_map/ppermute | solution.py:14
  37.7 2.0 %copy-start.4 = (f32[2,5,5]{2,0,1:T(2,128)S(1)}, f32[2,5,5]{2,0,1:T(2,128)}, u32[]{:S(2)}) copy-start(f32[2,5,5]{2,0,1:T(2,128)} %param.21) | copy-start | bytes 604
  40.8 6.1 %collective-permute-start.4 = (f32[5,2,3,128]{3,0,2,1:T(8,128)S(1)}, f32[5,2,3,128]{3,0,2,1:T(8,128)S(1)}, u32[]{:S(2)}, u32[]{:S(2)}) collective-permute-start(f32[5,2,3,128]{3,0,2,1:T(8,128)S(1)} %get-tuple-element.24), channel_id=1, source_target_pairs={{0,2},{2,4},{4,6},{1,3},{3,5},{5,7},{8,10},{10,12},{12,14},{9,11},... | collective-permute-start | bytes 46088 | tf_op jit(solution)/shard_map/ppermute | solution.py:14
  45.4 5.7 %collective-permute-start.5 = (f32[5,2,3,128]{3,0,2,1:T(8,128)S(1)}, f32[5,2,3,128]{3,0,2,1:T(8,128)S(1)}, u32[]{:S(2)}, u32[]{:S(2)}) collective-permute-start(f32[5,2,3,128]{3,0,2,1:T(8,128)S(1)} %get-tuple-element.25), channel_id=1, source_target_pairs={{2,0},{4,2},{6,4},{3,1},{5,3},{7,5},{10,8},{12,10},{14,12},{11,9},... | collective-permute-start | bytes 46088 | tf_op jit(solution)/shard_map/ppermute | solution.py:17
  51.6 7.2 %collective-permute-start.6 = (f32[5,2,70,3]{2,1,3,0:T(2,128)S(1)}, f32[5,2,70,3]{2,1,3,0:T(2,128)S(1)}, u32[]{:S(2)}, u32[]{:S(2)}) collective-permute-start(f32[5,2,70,3]{2,1,3,0:T(2,128)S(1)} %copy.73), channel_id=1, source_target_pairs={{1,0},{3,2},{5,4},{7,6},{9,8},{11,10},{13,12},{15,14},{17,16},{19,... | collective-permute-start | bytes 25208 | tf_op jit(solution)/shard_map/ppermute | solution.py:17
  53.1 6.0 %collective-permute-start.7 = (f32[5,2,70,3]{2,1,3,0:T(2,128)S(1)}, f32[5,2,70,3]{2,1,3,0:T(2,128)S(1)}, u32[]{:S(2)}, u32[]{:S(2)}) collective-permute-start(f32[5,2,70,3]{2,1,3,0:T(2,128)S(1)} %copy.75), channel_id=1, source_target_pairs={{0,1},{2,3},{4,5},{6,7},{8,9},{10,11},{12,13},{14,15},{16,17},{18,... | collective-permute-start | bytes 25208 | tf_op jit(solution)/shard_map/ppermute | solution.py:14
  59.8 1.2 %copy-start.3 = (f32[5,2,65,128]{3,0,2,1:T(8,128)S(1)}, f32[5,2,65,128]{3,0,2,1:T(8,128)}, u32[]{:S(2)}) copy-start(f32[5,2,65,128]{3,0,2,1:T(8,128)} %subtract_multiply_fusion.4) | copy-start | bytes 998404
  61.9 5.0 %collective-permute-start.8 = (f32[5,2,3,128]{3,0,2,1:T(8,128)S(1)}, f32[5,2,3,128]{3,0,2,1:T(8,128)S(1)}, u32[]{:S(2)}, u32[]{:S(2)}) collective-permute-start(f32[5,2,3,128]{3,0,2,1:T(8,128)S(1)} %get-tuple-element.22), channel_id=1, source_target_pairs={{0,2},{2,4},{4,6},{1,3},{3,5},{5,7},{8,10},{10,12},{12,14},{9,11},... | collective-permute-start | bytes 46088 | tf_op jit(solution)/shard_map/ppermute | solution.py:14
  65.4 5.7 %collective-permute-start.9 = (f32[5,2,3,128]{3,0,2,1:T(8,128)S(1)}, f32[5,2,3,128]{3,0,2,1:T(8,128)S(1)}, u32[]{:S(2)}, u32[]{:S(2)}) collective-permute-start(f32[5,2,3,128]{3,0,2,1:T(8,128)S(1)} %get-tuple-element.23), channel_id=1, source_target_pairs={{2,0},{4,2},{6,4},{3,1},{5,3},{7,5},{10,8},{12,10},{14,12},{11,9},... | collective-permute-start | bytes 46088 | tf_op jit(solution)/shard_map/ppermute | solution.py:17
  71.6 6.4 %collective-permute-start.10 = (f32[5,2,70,3]{2,1,3,0:T(2,128)S(1)}, f32[5,2,70,3]{2,1,3,0:T(2,128)S(1)}, u32[]{:S(2)}, u32[]{:S(2)}) collective-permute-start(f32[5,2,70,3]{2,1,3,0:T(2,128)S(1)} %copy.79), channel_id=1, source_target_pairs={{1,0},{3,2},{5,4},{7,6},{9,8},{11,10},{13,12},{15,14},{17,16},{19,... | collective-permute-start | bytes 25208 | tf_op jit(solution)/shard_map/ppermute | solution.py:17
  73.1 6.0 %collective-permute-start.11 = (f32[5,2,70,3]{2,1,3,0:T(2,128)S(1)}, f32[5,2,70,3]{2,1,3,0:T(2,128)S(1)}, u32[]{:S(2)}, u32[]{:S(2)}) collective-permute-start(f32[5,2,70,3]{2,1,3,0:T(2,128)S(1)} %copy.81), channel_id=1, source_target_pairs={{0,1},{2,3},{4,5},{6,7},{8,9},{10,11},{12,13},{14,15},{16,17},{18,... | collective-permute-start | bytes 25208 | tf_op jit(solution)/shard_map/ppermute | solution.py:14
where the time goes:
time: 83.3 us; the launch traced here: 82.7 us
  starting transfers between devices  34.5 us (41%)
  local copies, waits for them, and re-layouts  23.7 us (28%)
  other arithmetic  10.6 us (13%)
  waiting for transfers between devices  10.2 us (12%)
  matrix products  2.97 us (4%)
    ppermute x6, starting transfers between devices, extended(): lax.ppermute(lax.slice_in_dim(block, block.shape[dim] - width, None, axis...  26.8 us
    gather x12, local copies, waits for them, and re-layouts, strip_values(): picked = jnp.take(jnp.take(strip, rows, axis=2), cols, axis=3)  12 us
    ppermute x6, waiting for transfers between devices, extended(): lax.ppermute(lax.slice_in_dim(block, 0, width, axis=dim), axis, backward)  8.45 us
    ppermute x6, starting transfers between devices, extended(): lax.ppermute(lax.slice_in_dim(block, 0, width, axis=dim), axis, backward)  7.73 us
    div x6, other arithmetic, divergence(): flux = (wind * centered - jnp.abs(wind) * damping) / 60.0  6.05 us
    dot_general x3, matrix products, tendency(): jnp.einsum('lfg,glyx->flyx', coupling, center, precision=lax.Precision.HI...  2.97 us
    slice x6, local copies, waits for them, and re-layouts, extended(): lax.slice_in_dim(block, 0, width, axis=dim)  2.9 us
    unnamed x24, local copies, waits for them, and re-layouts  2.66 us
  transfers between devices with their start and end apart: 12, of which 6 were waited for; matrix products, arithmetic and copies ran while one was open for 28% of the time, Pallas kernels for 0%

commit v1 on v0

v1 whole, which is shorter than its diff:
```python
import functools

import jax
import jax.numpy as jnp
import numpy as np
from jax import lax
from jax.experimental import pallas as pl
from jax.experimental.pallas import tpu as pltpu
from jax.sharding import PartitionSpec as P

RELAX = 0.25
REACH = 3
HALO = 3 * REACH
PAD = 16
LANES = 128

UPWIND = (-2.0, 15.0, -60.0, 20.0, 30.0, -3.0, 0.0)
CENTRAL = (-1.0, 9.0, -45.0, 0.0, 45.0, -9.0, 1.0)
DAMPING = (1.0, -6.0, 15.0, -20.0, 15.0, -6.0, 1.0)


def band_matrices(width):
    bands = np.zeros((2, width, width), np.float32)
    for offset in range(-REACH, REACH + 1):
        for col in range(width):
            row = (col + offset) % width
            bands[0, row, col] = UPWIND[offset + REACH]
            bands[1, row, col] = -UPWIND[REACH - offset]
    return bands


def iota(shape, dim):
    return lax.broadcasted_iota(jnp.int32, shape, dim)


def edge_weight(distance, width):
    dist = distance.astype(jnp.float32)
    inside = (dist >= 0.0) & (dist < width)
    return jnp.where(inside, jnp.square((width - dist) / width), 0.0)


def pack_y_kernel(fields, to_north, to_south):
    count_f, count_l, rows, _ = fields.shape
    for f in range(count_f):
        for l in range(count_l):
            base = HALO * (f * count_l + l)
            to_north[base : base + HALO, :] = fields[f, l, 0:HALO, :]
            to_south[base : base + HALO, :] = fields[f, l, rows - HALO : rows, :]


def pack_x_kernel(gx_count, fields, from_north, from_south, *rest):
    outs, ext = rest[:-1], rest[-1]
    count_f, count_l, rows, cols = fields.shape
    ext_rows = ext.shape[0]
    lane = iota((ext_rows, LANES), 1)
    col_east, col_west = cols - HALO, 0
    if gx_count == 2:
        starts = [jnp.where(lax.axis_index("gx") == 0, col_east, col_west)]
    else:
        starts = [col_east, col_west]
    packed = [jnp.zeros((ext_rows, LANES), jnp.float32) for _ in starts]
    ext[...] = jnp.zeros_like(ext)
    for f in range(count_f):
        for l in range(count_l):
            slot = HALO * (f * count_l + l)
            ext[PAD - HALO : PAD, 0:cols] = from_north[slot : slot + HALO, :]
            ext[PAD : PAD + rows, 0:cols] = fields[f, l]
            ext[PAD + rows : PAD + rows + HALO, 0:cols] = from_south[slot : slot + HALO, :]
            whole = ext[...]
            for n, start in enumerate(starts):
                shift = lax.rem(slot + LANES - start, LANES)
                moved = pltpu.roll(whole, shift, 1)
                packed[n] = jnp.where((lane >= slot) & (lane < slot + HALO), moved, packed[n])
    for out, value in zip(outs, packed):
        out[...] = value


def step_kernel(
    grid_sizes,
    gx_recv,
    fields,
    from_north,
    from_south,
    *rest,
):
    gy_count, gx_count = grid_sizes
    side = rest[:gx_recv]
    (
        wind_x,
        wind_y,
        coupling,
        north,
        south,
        west,
        east,
        scale,
        widths,
        bands,
        out,
        q0,
        q1,
        q2,
        drive,
        relax,
        inside,
        xdiv,
    ) = rest[gx_recv:]
    count_f, count_l, rows, cols = fields.shape
    tiles, _, _, ext_rows, _ = q0.shape
    span = tiles * LANES
    last = tiles - 1
    strip = north.shape[2]
    total_rows, total_cols = rows * gy_count, cols * gx_count
    gy, gx = lax.axis_index("gy"), lax.axis_index("gx")
    row_start, col_start = gy * rows, gx * cols

    q0[...] = jnp.zeros_like(q0)
    lane = iota((ext_rows, LANES), 1)
    for f in range(count_f):
        for l in range(count_l):
            slot = HALO * (f * count_l + l)
            q0[0, f, l, PAD - HALO : PAD, 0:cols] = from_north[slot : slot + HALO, :]
            q0[0, f, l, PAD : PAD + rows, 0:cols] = fields[f, l]
            q0[0, f, l, PAD + rows : PAD + rows + HALO, 0:cols] = from_south[slot : slot + HALO, :]
            east_lane, west_lane = cols % LANES, LANES - HALO
            if gx_recv == 1:
                target = jnp.where(gx == 0, east_lane, west_lane)
                placed = [(side[0], target)]
            else:
                placed = [(side[0], west_lane), (side[1], east_lane)]
            merged = q0[last, f, l]
            for source, target in placed:
                moved = pltpu.roll(source[...], lax.rem(target + LANES - slot, LANES), 1)
                merged = jnp.where((lane >= target) & (lane < target + HALO), moved, merged)
            q0[last, f, l] = merged

    width = [widths[s].astype(jnp.float32) for s in range(4)]
    row_global = iota((ext_rows, LANES), 0) + (row_start - PAD)
    row_weight = edge_weight(row_global, width[0]) + edge_weight(
        total_rows - 1 - row_global, width[1]
    )
    row_inside = (row_global >= 0) & (row_global < total_rows)
    for t in range(tiles):
        pos = lane + t * LANES
        col_global = jnp.where(pos >= span - HALO, pos - span, pos) + col_start
        col_weight = edge_weight(col_global, width[2]) + edge_weight(
            total_cols - 1 - col_global, width[3]
        )
        relax[t] = RELAX * (row_weight + col_weight)
        inside[t] = jnp.where(
            row_inside & (col_global >= 0) & (col_global < total_cols), 1.0, 0.0
        )

    drive[...] = jnp.zeros_like(drive)
    pos = iota((strip, LANES), 1)
    depth = iota((strip, LANES), 0)
    pick = jnp.concatenate([pos == depth, pos == depth + (cols - strip)], axis=0).astype(
        jnp.float32
    ).astype(jnp.bfloat16)
    lane8 = iota((8, LANES), 1)
    west_weight = RELAX * edge_weight(lane8 + col_start, width[2])
    east_weight = RELAX * edge_weight(total_cols - 1 - (lane8 + col_start), width[3])
    west_weight = jnp.where(lane8 < strip, west_weight, 0.0)
    east_weight = jnp.where((lane8 >= cols - strip) & (lane8 < cols), east_weight, 0.0)
    shift = lax.rem(PAD + total_rows - row_start, total_rows)
    for f in range(count_f):
        for l in range(count_l):
            both = jnp.concatenate([west[f, l], east[f, l]], axis=0).astype(jnp.float32)
            both = pltpu.roll(both, shift, 1)[:, 0:LANES].astype(jnp.bfloat16)
            raw = lax.dot_general(
                both, pick, (((0,), (0,)), ((), ())), preferred_element_type=jnp.float32
            )
            factor = west_weight * scale[2, l, f] + east_weight * scale[3, l, f]
            drive[0, f, l] = raw[0:ext_rows] * factor[0:1, :]

    shift = lax.rem(total_cols - col_start, total_cols)
    strip_lane = iota((strip, LANES), 1)
    strip_row = iota((strip, LANES), 0)
    for source, side_id, at, here in (
        (north, 0, PAD, gy == 0),
        (south, 1, PAD + rows - strip, gy == gy_count - 1),
    ):

        @pl.when(here)
        def _(source=source, side_id=side_id, at=at):
            distance = strip_row if side_id == 0 else strip - 1 - strip_row
            weight = RELAX * edge_weight(distance, width[side_id])
            for f in range(count_f):
                for l in range(count_l):
                    values = pltpu.roll(source[f, l].astype(jnp.float32), shift, 1)
                    factor = weight * scale[side_id, l, f]
                    for t in range(tiles):
                        part = values[:, t * LANES : (t + 1) * LANES]
                        if t == last:
                            wrapped = values[:, total_cols - LANES : total_cols]
                            part = jnp.where(strip_lane >= LANES - HALO, wrapped, part)
                        old = drive[t, f, l, at : at + strip, :]
                        drive[t, f, l, at : at + strip, :] = old + factor * part

    def section(src, base, dst, fac, first, groups, out_tiles):
        for l in range(count_l):
            c_x, c_y = wind_x[l], wind_y[l]
            band = bands[jnp.where(c_x < 0.0, 1, 0)]
            height = groups * 8
            flat = [
                src[t, :, l, first : first + height, :].reshape(count_f * height, LANES)
                for t in range(tiles)
            ]
            state = jnp.concatenate(flat, axis=1) if tiles > 1 else flat[0]
            high = state.astype(jnp.bfloat16)
            low = (state - high.astype(jnp.float32)).astype(jnp.bfloat16)
            band = band[:, 0 : out_tiles * LANES]
            moved = jnp.dot(high, band, preferred_element_type=jnp.float32) + jnp.dot(
                low, band, preferred_element_type=jnp.float32
            )
            for t in range(out_tiles):
                xdiv[t, :, 0:height, :] = moved[:, t * LANES : (t + 1) * LANES].reshape(
                    count_f, height, LANES
                )
            scaled_y, scaled_abs = fac / 60.0 * c_y, fac / 60.0 * jnp.abs(c_y)
            scaled_x = fac / 60.0 * c_x
            taps = [
                scaled_abs * DAMPING[k] - scaled_y * CENTRAL[k] for k in range(2 * REACH + 1)
            ]
            mix = [
                [
                    fac * coupling[f, l, g] + (taps[REACH] if f == g else 0.0)
                    for g in range(count_f)
                ]
                for f in range(count_f)
            ]

            def group(n, _):
                at = pl.multiple_of(first + n * 8, 8)
                local = pl.multiple_of(n * 8, 8)
                for t in range(out_tiles):
                    center = [src[t, g, l, pl.ds(at, 8), :] for g in range(count_f)]
                    weight = relax[t, pl.ds(at, 8), :]
                    for f in range(count_f):
                        rate = drive[t, f, l, pl.ds(at, 8), :] - weight * center[f]
                        total = fac * rate - scaled_x * xdiv[t, f, pl.ds(local, 8), :]
                        for g in range(count_f):
                            total = total + mix[f][g] * center[g]
                        for k in range(2 * REACH + 1):
                            if k != REACH:
                                total = total + taps[k] * src[
                                    t, f, l, pl.ds(at + (k - REACH), 8), :
                                ]
                        value = base[t, f, l, pl.ds(at, 8), :] + total
                        if dst is out:
                            out[f, l, pl.ds(local, 8), :] = value[:, 0:cols]
                        else:
                            dst[t, f, l, pl.ds(at, 8), :] = value * inside[t, pl.ds(at, 8), :]
                return 0

            lax.fori_loop(0, groups, group, 0)

    wide = (rows + 16) // 8
    q1[...] = jnp.zeros_like(q1)
    q2[...] = jnp.zeros_like(q2)
    section(q0, q0, q1, 1.0 / 3.0, PAD - 8, wide, tiles)
    section(q1, q0, q2, 0.5, PAD - 8, wide, tiles)
    section(q2, q0, out, 1.0, PAD, rows // 8, 1)


def swap_rounds(count):
    forward = [(i, i + 1) for i in range(count - 1)]
    return forward, [(b, a) for a, b in forward]


def local(gy_count, gx_count, fields, wind_x, wind_y, coupling, north, south, west, east, strip_scale, widths):
    count_f, count_l, rows, cols = fields.shape
    ext_rows = rows + 2 * PAD
    tiles = 1 if cols + 2 * HALO <= LANES else 2
    packed_rows = -(-HALO * count_f * count_l // 8) * 8
    vmem = pl.BlockSpec(memory_space=pltpu.VMEM)
    smem = pl.BlockSpec(memory_space=pltpu.SMEM)

    strip_shape = jax.ShapeDtypeStruct((packed_rows, cols), jnp.float32)
    to_north, to_south = pl.pallas_call(
        pack_y_kernel,
        out_shape=(strip_shape, strip_shape),
        in_specs=[vmem],
        out_specs=(vmem, vmem),
        name="pack_y",
    )(fields)
    forward, backward = swap_rounds(gy_count)
    from_north = lax.ppermute(to_south, "gy", forward)
    from_south = lax.ppermute(to_north, "gy", backward)

    recv_count = 1 if gx_count == 2 else 2
    side_shape = jax.ShapeDtypeStruct((ext_rows, LANES), jnp.float32)
    sent = pl.pallas_call(
        functools.partial(pack_x_kernel, gx_count),
        out_shape=(side_shape,) * recv_count,
        in_specs=[vmem] * 3,
        out_specs=(vmem,) * recv_count,
        scratch_shapes=[pltpu.VMEM((ext_rows, LANES), jnp.float32)],
        name="pack_x",
    )(fields, from_north, from_south)
    forward, backward = swap_rounds(gx_count)
    if recv_count == 1:
        side = [lax.ppermute(sent[0], "gx", forward + backward)]
    else:
        side = [lax.ppermute(sent[0], "gx", forward), lax.ppermute(sent[1], "gx", backward)]

    state = pltpu.VMEM((tiles, count_f, count_l, ext_rows, LANES), jnp.float32)
    plane = pltpu.VMEM((tiles, ext_rows, LANES), jnp.float32)
    bands = jnp.asarray(band_matrices(tiles * LANES), jnp.bfloat16)
    return pl.pallas_call(
        functools.partial(step_kernel, (gy_count, gx_count), recv_count),
        out_shape=jax.ShapeDtypeStruct(fields.shape, jnp.float32),
        in_specs=[vmem] * (3 + recv_count) + [smem] * 3 + [vmem] * 4 + [smem] * 2 + [vmem],
        out_specs=vmem,
        scratch_shapes=[
            state,
            state,
            state,
            state,
            plane,
            plane,
            pltpu.VMEM((tiles, count_f, rows + 16, LANES), jnp.float32),
        ],
        name="three_sections",
    )(
        fields,
        from_north,
        from_south,
        *side,
        wind_x,
        wind_y,
        jnp.transpose(coupling, (1, 0, 2)),
        north,
        south,
        jnp.swapaxes(west, 2, 3),
        jnp.swapaxes(east, 2, 3),
        jnp.transpose(strip_scale, (0, 2, 1)),
        widths,
        bands,
    )


def solution(mesh):
    return jax.shard_map(
        functools.partial(local, mesh.shape["gy"], mesh.shape["gx"]),
        mesh=mesh,
        in_specs=(
            P("mem", None, "gy", "gx"),
            P("mem"),
            P("mem"),
            P(),
            P("mem", None, None, None),
            P("mem", None, None, None),
            P("mem", None, None, None),
            P("mem", None, None, None),
            P("mem", None, None),
            P(),
        ),
        out_specs=P("mem", None, "gy", "gx"),
        check_vma=False,
    )
```

time: 83.3 us -> 27.9 us (0.33)
  starting transfers between devices: 34.5 us -> 7.73 us
  local copies, waits for them, and re-layouts: 23.7 us -> 1.23 us
  Pallas kernels: 0 us -> 11 us
  other arithmetic: 10.6 us -> 0 us
  matrix products: 2.97 us -> 0 us
  waiting for transfers between devices: 10.2 us -> 7.7 us
    ppermute x12 -> x3, starting transfers between devices: 34.5 us -> 7.73 us  [the longest x1 4.95 us: local(): from_north = lax.ppermute(to_south, 'gy', forward)]
    gather x12 -> x0, local copies, waits for them, and re-layouts: 12 us -> none  [strip_values(): picked = jnp.take(jnp.take(strip, rows, axis=2), cols, axis=3)]
    pallas_call x0 -> x3, Pallas kernels: none -> 11 us  [the longest x1 7.57 us: local(): pl.pallas_call(functools.partial(step_kernel, (gy_count, gx_count), recv_...]
    div x6 -> x0, other arithmetic: 6.05 us -> none  [divergence(): flux = (wind * centered - jnp.abs(wind) * damping) / 60.0]
    slice x13 -> x0, local copies, waits for them, and re-layouts: 5.13 us -> none  [the longest x6 2.9 us: extended(): lax.slice_in_dim(block, 0, width, axis=dim)]
    dot_general x3 -> x0, matrix products: 2.97 us -> none  [tendency(): jnp.einsum('lfg,glyx->flyx', coupling, center, precision=lax.Precision.HI...]
    ppermute x12 -> x3, waiting for transfers between devices: 10.2 us -> 7.7 us  [the longest x1 4.14 us: local(): from_south = lax.ppermute(to_north, 'gy', backward)]
    select_n x9 -> x0, other arithmetic: 1.84 us -> none  [the longest x1 1.22 us: profile(): jnp.where((dist_float >= 0.0) & (dist_float < width), jnp.square((width -...]
  transfers between devices with their start and end apart: 12 -> 3, of which waited for: 6 -> 3; matrix products, arithmetic and copies ran while one was open for 28% -> 0% of each run, Pallas kernels for 0% -> 0%
where the time goes in v1:
time: 27.9 us; the launch traced here: 27.7 us
  Pallas kernels  11 us (39%)
  starting transfers between devices  7.73 us (28%)
  waiting for transfers between devices  7.7 us (28%)
  local copies, waits for them, and re-layouts  1.23 us (4%)
    pallas_call x1, Pallas kernels, local(): pl.pallas_call(functools.partial(step_kernel, (gy_count, gx_count), recv_...  7.57 us
    ppermute x1, starting transfers between devices, local(): from_north = lax.ppermute(to_south, 'gy', forward)  4.95 us
    ppermute x1, waiting for transfers between devices, local(): from_south = lax.ppermute(to_north, 'gy', backward)  4.14 us
    ppermute x1, waiting for transfers between devices, local(): side = [lax.ppermute(sent[0], 'gx', forward + backward)]  2.81 us
    pallas_call x1, Pallas kernels, local(): pl.pallas_call(functools.partial(pack_x_kernel, gx_count), out_shape=(sid...  1.84 us
    pallas_call x1, Pallas kernels, local(): pl.pallas_call(pack_y_kernel, out_shape=(strip_shape, strip_shape), in_sp...  1.61 us
    ppermute x1, starting transfers between devices, local(): side = [lax.ppermute(sent[0], 'gx', forward + backward)]  1.49 us
    ppermute x1, starting transfers between devices, local(): from_south = lax.ppermute(to_north, 'gy', backward)  1.29 us
  transfers between devices with their start and end apart: 3, of which 3 were waited for; matrix products, arithmetic and copies ran while one was open for 0% of the time, Pallas kernels for 0%

profile of v1, /device:TPU:0, one launch (start us, length us, event | category | flops | bytes accessed | tf_op | source)
XLA Modules:
  0.0 27.7 jit_solution(15185720348619763534)
XLA Ops:
  0.0 1.6 %pack_y.1 = (f32[96,128]{1,0:T(8,128)}, f32[96,128]{1,0:T(8,128)}) custom-call(f32[5,2,64,128]{3,2,1,0:T(8,128)} %fields.5), custom_call_target="tpu_custom_call" | custom-call | tf_op jit(solution)/shard_map/pack_y/pallas_call | solution.py:280
  1.6 4.9 %collective-permute-start = (f32[96,128]{1,0:T(8,128)}, f32[96,128]{1,0:T(8,128)S(1)}, u32[]{:S(2)}, u32[]{:S(2)}) collective-permute-start(f32[96,128]{1,0:T(8,128)} %get-tuple-element.7), channel_id=1, source_target_pairs={{0,2},{2,4},{4,6},{1,3},{3,5},{5,7},{8,10},{10,12},{12,14},{9,11},... | collective-permute-start | bytes 147464 | tf_op jit(solution)/shard_map/ppermute | solution.py:288
  6.6 1.3 %collective-permute-start.1 = (f32[96,128]{1,0:T(8,128)}, f32[96,128]{1,0:T(8,128)S(1)}, u32[]{:S(2)}, u32[]{:S(2)}) collective-permute-start(f32[96,128]{1,0:T(8,128)} %get-tuple-element.8), channel_id=1, source_target_pairs={{2,0},{4,2},{6,4},{3,1},{5,3},{7,5},{10,8},{12,10},{14,12},{11,9},... | collective-permute-start | bytes 147464 | tf_op jit(solution)/shard_map/ppermute | solution.py:289
  7.9 0.7 %collective-permute-done.from_north = f32[96,128]{1,0:T(8,128)S(1)} collective-permute-done((f32[96,128]{1,0:T(8,128)}, f32[96,128]{1,0:T(8,128)S(1)}, u32[]{:S(2)}, u32[]{:S(2)}) %collective-permute-start) | collective-permute-done | bytes 49184 | tf_op jit(solution)/shard_map/ppermute | solution.py:288
  8.6 0.0 copy-start
  8.6 4.1 %collective-permute-done.1.from_south = f32[96,128]{1,0:T(8,128)S(1)} collective-permute-done((f32[96,128]{1,0:T(8,128)}, f32[96,128]{1,0:T(8,128)S(1)}, u32[]{:S(2)}, u32[]{:S(2)}) %collective-permute-start.1) | collective-permute-done | bytes 49184 | tf_op jit(solution)/shard_map/ppermute | solution.py:289
  12.8 0.0 copy-done
  12.8 0.0 copy-start.1
  12.8 0.6 %copy-done.1 = f32[96,128]{1,0:T(8,128)} copy-done((f32[96,128]{1,0:T(8,128)}, f32[96,128]{1,0:T(8,128)S(1)}, u32[]{:S(2)}) %copy-start.1) | copy-done | bytes 49176
  13.4 1.8 %pack_x.1 = f32[96,128]{1,0:T(8,128)} custom-call(f32[5,2,64,128]{3,2,1,0:T(8,128)} %fields.5, f32[96,128]{1,0:T(8,128)} %copy-done, f32[96,128]{1,0:T(8,128)} %copy-done.1), custom_call_target="tpu_custom_call" | custom-call | tf_op jit(solution)/shard_map/pack_x/pallas_call | solution.py:293
  15.2 1.5 %collective-permute-start.2 = (f32[96,128]{1,0:T(8,128)}, f32[96,128]{1,0:T(8,128)S(1)}, u32[]{:S(2)}, u32[]{:S(2)}) collective-permute-start(f32[96,128]{1,0:T(8,128)} %pack_x.1), channel_id=1, source_target_pairs={{0,1},{1,0},{2,3},{3,2},{4,5},{5,4},{6,7},{7,6},{8,9},{9,8},{10,11... | collective-permute-start | bytes 147464 | tf_op jit(solution)/shard_map/ppermute | solution.py:303
  16.7 2.8 %collective-permute-done.2.rest_0_ = f32[96,128]{1,0:T(8,128)S(1)} collective-permute-done((f32[96,128]{1,0:T(8,128)}, f32[96,128]{1,0:T(8,128)S(1)}, u32[]{:S(2)}, u32[]{:S(2)}) %collective-permute-start.2) | collective-permute-done | bytes 49184 | tf_op jit(solution)/shard_map/ppermute | solution.py:303
  19.5 0.0 copy-start.2
  19.5 0.6 %copy-done.2 = f32[96,128]{1,0:T(8,128)} copy-done((f32[96,128]{1,0:T(8,128)}, f32[96,128]{1,0:T(8,128)S(1)}, u32[]{:S(2)}) %copy-start.2) | copy-done | bytes 49176
  20.1 7.6 %three_sections.1 = f32[5,2,64,128]{3,2,1,0:T(8,128)} custom-call(f32[5,2,64,128]{3,2,1,0:T(8,128)} %fields.5, f32[96,128]{1,0:T(8,128)} %copy-done, f32[96,128]{1,0:T(8,128)} %copy-done.1, f32[96,128]{1,0:T(8,128)} %copy-done.2, f32[2]{0:T(128)} %rest_1_.1, f32[2]{0:T(128)} %rest_2_.1, f32[5,2,5]{2,1,0:T(2,128)} %bitcast.6, bf16[5,2,8,256]{3,2,1,0:T(8,128)(2,1)} %rest_4_.1, ...), custom_call_target="tpu_custom_call" | custom-call | tf_op jit(solution)/shard_map/three_sections/pallas_call | solution.py:310
Async XLA Ops:
  1.6 7.0 %collective-permute-start = (f32[96,128]{1,0:T(8,128)}, f32[96,128]{1,0:T(8,128)S(1)}, u32[]{:S(2)}, u32[]{:S(2)}) collective-permute-start(f32[96,128]{1,0:T(8,128)} %get-tuple-element.7), channel_id=1, source_target_pairs={{0,2},{2,4},{4,6},{1,3},{3,5},{5,7},{8,10},{10,12},{12,14},{9,11},... | collective-permute-start | bytes 147464 | tf_op jit(solution)/shard_map/ppermute | solution.py:288
  6.6 6.2 %collective-permute-start.1 = (f32[96,128]{1,0:T(8,128)}, f32[96,128]{1,0:T(8,128)S(1)}, u32[]{:S(2)}, u32[]{:S(2)}) collective-permute-start(f32[96,128]{1,0:T(8,128)} %get-tuple-element.8), channel_id=1, source_target_pairs={{2,0},{4,2},{6,4},{3,1},{5,3},{7,5},{10,8},{12,10},{14,12},{11,9},... | collective-permute-start | bytes 147464 | tf_op jit(solution)/shard_map/ppermute | solution.py:289
  8.6 4.1 %copy-start = (f32[96,128]{1,0:T(8,128)}, f32[96,128]{1,0:T(8,128)S(1)}, u32[]{:S(2)}) copy-start(f32[96,128]{1,0:T(8,128)S(1)} %collective-permute-done.from_north) | copy-start | bytes 147460
  12.8 0.6 %copy-start.1 = (f32[96,128]{1,0:T(8,128)}, f32[96,128]{1,0:T(8,128)S(1)}, u32[]{:S(2)}) copy-start(f32[96,128]{1,0:T(8,128)S(1)} %collective-permute-done.1.from_south) | copy-start | bytes 147460
  15.2 4.3 %collective-permute-start.2 = (f32[96,128]{1,0:T(8,128)}, f32[96,128]{1,0:T(8,128)S(1)}, u32[]{:S(2)}, u32[]{:S(2)}) collective-permute-start(f32[96,128]{1,0:T(8,128)} %pack_x.1), channel_id=1, source_target_pairs={{0,1},{1,0},{2,3},{3,2},{4,5},{5,4},{6,7},{7,6},{8,9},{9,8},{10,11... | collective-permute-start | bytes 147464 | tf_op jit(solution)/shard_map/ppermute | solution.py:303
  19.5 0.6 %copy-start.2 = (f32[96,128]{1,0:T(8,128)}, f32[96,128]{1,0:T(8,128)S(1)}, u32[]{:S(2)}) copy-start(f32[96,128]{1,0:T(8,128)S(1)} %collective-permute-done.2.rest_0_) | copy-start | bytes 147460

commit v2 on v1

--- a/solution.py
+++ b/solution.py
@@ -282,6 +282,7 @@
         out_shape=(strip_shape, strip_shape),
         in_specs=[vmem],
         out_specs=(vmem, vmem),
+        compiler_params=pltpu.CompilerParams(vmem_limit_bytes=4 << 20),
         name="pack_y",
     )(fields)
     forward, backward = swap_rounds(gy_count)
@@ -296,6 +297,7 @@
         in_specs=[vmem] * 3,
         out_specs=(vmem,) * recv_count,
         scratch_shapes=[pltpu.VMEM((ext_rows, LANES), jnp.float32)],
+        compiler_params=pltpu.CompilerParams(vmem_limit_bytes=4 << 20),
         name="pack_x",
     )(fields, from_north, from_south)
     forward, backward = swap_rounds(gx_count)
@@ -321,6 +323,7 @@
             plane,
             pltpu.VMEM((tiles, count_f, rows + 16, LANES), jnp.float32),
         ],
+        compiler_params=pltpu.CompilerParams(vmem_limit_bytes=16 << 20),
         name="three_sections",
     )(
         fields,

time: 27.9 us -> 24.6 us (0.88)
  Pallas kernels: 11 us -> 7.28 us
  waiting for transfers between devices: 7.7 us -> 7.28 us
  local copies, waits for them, and re-layouts: 1.23 us -> 1.63 us
  starting transfers between devices: 7.73 us -> 8.07 us
    pallas_call x1, Pallas kernels: 1.84 us -> 0.21 us  [local(): pl.pallas_call(functools.partial(pack_x_kernel, gx_count), out_shape=(sid...]
    pallas_call x1, Pallas kernels: 1.61 us -> 0.01 us  [local(): pl.pallas_call(pack_y_kernel, out_shape=(strip_shape, strip_shape), in_sp...]
    pallas_call x1, Pallas kernels: 7.57 us -> 7.05 us  [local(): pl.pallas_call(functools.partial(step_kernel, (gy_count, gx_count), recv_...]
    ppermute x1, waiting for transfers between devices: 0.75 us -> 0.25 us  [local(): from_north = lax.ppermute(to_south, 'gy', forward)]
    unnamed x6 -> x24, local copies, waits for them, and re-layouts: 1.23 us -> 1.63 us
    ppermute x1, waiting for transfers between devices: 4.14 us -> 4.43 us  [local(): from_south = lax.ppermute(to_north, 'gy', backward)]
where the time goes in v2:
time: 24.6 us; the launch traced here: 24.4 us
  starting transfers between devices  8.07 us (33%)
  Pallas kernels  7.28 us (30%)
  waiting for transfers between devices  7.28 us (30%)
  local copies, waits for them, and re-layouts  1.63 us (7%)
    pallas_call x1, Pallas kernels, local(): pl.pallas_call(functools.partial(step_kernel, (gy_count, gx_count), recv_...  7.05 us
    ppermute x1, starting transfers between devices, local(): from_north = lax.ppermute(to_south, 'gy', forward)  5.09 us
    ppermute x1, waiting for transfers between devices, local(): from_south = lax.ppermute(to_north, 'gy', backward)  4.43 us
    ppermute x1, waiting for transfers between devices, local(): side = [lax.ppermute(sent[0], 'gx', forward + backward)]  2.6 us
    unnamed x24, local copies, waits for them, and re-layouts  1.63 us
    ppermute x1, starting transfers between devices, local(): side = [lax.ppermute(sent[0], 'gx', forward + backward)]  1.56 us
    ppermute x1, starting transfers between devices, local(): from_south = lax.ppermute(to_north, 'gy', backward)  1.42 us
  transfers between devices with their start and end apart: 3, of which 3 were waited for; matrix products, arithmetic and copies ran while one was open for 0% of the time, Pallas kernels for 0%

profile of v2, /device:TPU:0, one launch (start us, length us, event | category | flops | bytes accessed | tf_op | source)
XLA Modules:
  0.0 24.4 jit_solution(10867045429690453138)
XLA Ops:
  0.0 0.0 copy-start
  0.0 1.0 %copy-done = f32[5,2,64,128]{3,2,1,0:T(8,128)S(1)} copy-done((f32[5,2,64,128]{3,2,1,0:T(8,128)S(1)}, f32[5,2,64,128]{3,2,1,0:T(8,128)}, u32[]{:S(2)}) %copy-start) | copy-done | bytes 327704
  1.0 0.0 copy-start.1
  1.0 0.0 copy-start.2
  1.0 5.1 %collective-permute-start = (f32[96,128]{1,0:T(8,128)S(1)}, f32[96,128]{1,0:T(8,128)S(1)}, u32[]{:S(2)}, u32[]{:S(2)}) collective-permute-start(f32[96,128]{1,0:T(8,128)S(1)} %get-tuple-element.7), channel_id=1, source_target_pairs={{0,2},{2,4},{4,6},{1,3},{3,5},{5,7},{8,10},{10,12},{12,14},{9,11},... | collective-permute-start | bytes 147464 | tf_op jit(solution)/shard_map/ppermute | solution.py:289
  6.1 0.0 copy-start.3
  6.1 0.0 copy-start.4
  6.1 0.0 copy-start.5
  6.1 0.0 copy-start.6
  6.1 1.4 %collective-permute-start.1 = (f32[96,128]{1,0:T(8,128)S(1)}, f32[96,128]{1,0:T(8,128)S(1)}, u32[]{:S(2)}, u32[]{:S(2)}) collective-permute-start(f32[96,128]{1,0:T(8,128)S(1)} %get-tuple-element.8), channel_id=1, source_target_pairs={{2,0},{4,2},{6,4},{3,1},{5,3},{7,5},{10,8},{12,10},{14,12},{11,9},... | collective-permute-start | bytes 147464 | tf_op jit(solution)/shard_map/ppermute | solution.py:290
  7.6 0.3 %collective-permute-done.from_north = f32[96,128]{1,0:T(8,128)S(1)} collective-permute-done((f32[96,128]{1,0:T(8,128)S(1)}, f32[96,128]{1,0:T(8,128)S(1)}, u32[]{:S(2)}, u32[]{:S(2)}) %collective-permute-start) | collective-permute-done | bytes 49184 | tf_op jit(solution)/shard_map/ppermute | solution.py:289
  7.8 4.4 %collective-permute-done.1.from_south = f32[96,128]{1,0:T(8,128)S(1)} collective-permute-done((f32[96,128]{1,0:T(8,128)S(1)}, f32[96,128]{1,0:T(8,128)S(1)}, u32[]{:S(2)}, u32[]{:S(2)}) %collective-permute-start.1) | collective-permute-done | bytes 49184 | tf_op jit(solution)/shard_map/ppermute | solution.py:290
  12.3 0.0 copy-start.8
  12.3 0.2 pack_x.1
  12.5 0.0 copy-start.7
  12.5 1.6 %collective-permute-start.2 = (f32[96,128]{1,0:T(8,128)S(1)}, f32[96,128]{1,0:T(8,128)S(1)}, u32[]{:S(2)}, u32[]{:S(2)}) collective-permute-start(f32[96,128]{1,0:T(8,128)S(1)} %pack_x.1), channel_id=1, source_target_pairs={{0,1},{1,0},{2,3},{3,2},{4,5},{5,4},{6,7},{7,6},{8,9},{9,8},{10,11... | collective-permute-start | bytes 147464 | tf_op jit(solution)/shard_map/ppermute | solution.py:305
  14.1 2.6 %collective-permute-done.2.rest_0_ = f32[96,128]{1,0:T(8,128)S(1)} collective-permute-done((f32[96,128]{1,0:T(8,128)S(1)}, f32[96,128]{1,0:T(8,128)S(1)}, u32[]{:S(2)}, u32[]{:S(2)}) %collective-permute-start.2) | collective-permute-done | bytes 49184 | tf_op jit(solution)/shard_map/ppermute | solution.py:305
  16.7 0.0 copy-start.9
  16.7 0.0 copy-start.10
  16.7 0.0 copy-start.11
  16.7 0.0 copy-done.1
  16.7 0.0 copy-done.2
  16.7 0.0 copy-done.3
  16.7 0.0 copy-done.4
  16.7 0.0 copy-done.5
  16.7 0.0 copy-done.6
  16.7 0.0 copy-done.8
  16.7 0.0 copy-done.7
  16.7 0.6 %copy-done.9 = f32[2]{0:T(128)S(1)} copy-done((f32[2]{0:T(128)S(1)}, f32[2]{0:T(128)}, u32[]{:S(2)}) %copy-start.9) | copy-done | bytes 32
  17.3 0.0 copy-done.10
  17.3 0.0 copy-done.11
  17.3 7.1 %three_sections.1 = f32[5,2,64,128]{3,2,1,0:T(8,128)} custom-call(f32[5,2,64,128]{3,2,1,0:T(8,128)S(1)} %copy-done.1, f32[96,128]{1,0:T(8,128)S(1)} %collective-permute-done.from_north, f32[96,128]{1,0:T(8,128)S(1)} %collective-permute-done.1.from_south, f32[96,128]{1,0:T(8,128)S(1)} %collective-permute-done.2.rest_0_, f32[2]{0:T(128)S(1)} %copy-done.9, ...), custom_call_target="tpu_custom_call" | custom-call | tf_op jit(solution)/shard_map/three_sections/pallas_call | solution.py:312
  (1 shorter events, 0.0 us)
Async XLA Ops:
  0.0 1.0 %copy-start = (f32[5,2,64,128]{3,2,1,0:T(8,128)S(1)}, f32[5,2,64,128]{3,2,1,0:T(8,128)}, u32[]{:S(2)}) copy-start(f32[5,2,64,128]{3,2,1,0:T(8,128)} %fields.5) | copy-start | bytes 983044
  1.0 15.7 %copy-start.1 = (f32[5,2,64,128]{3,2,1,0:T(8,128)S(1)}, f32[5,2,64,128]{3,2,1,0:T(8,128)}, u32[]{:S(2)}) copy-start(f32[5,2,64,128]{3,2,1,0:T(8,128)} %fields.5) | copy-start | bytes 983044
  1.0 15.7 %copy-start.2 = (bf16[2,256,256]{2,1,0:T(8,128)(2,1)S(1)}, bf16[2,256,256]{2,1,0:T(8,128)(2,1)}, u32[]{:S(2)}) copy-start(bf16[2,256,256]{2,1,0:T(8,128)(2,1)} %constant.2.clone.rest_10_) | copy-start | bytes 786436
  1.0 6.8 %collective-permute-start = (f32[96,128]{1,0:T(8,128)S(1)}, f32[96,128]{1,0:T(8,128)S(1)}, u32[]{:S(2)}, u32[]{:S(2)}) collective-permute-start(f32[96,128]{1,0:T(8,128)S(1)} %get-tuple-element.7), channel_id=1, source_target_pairs={{0,2},{2,4},{4,6},{1,3},{3,5},{5,7},{8,10},{10,12},{12,14},{9,11},... | collective-permute-start | bytes 147464 | tf_op jit(solution)/shard_map/ppermute | solution.py:289
  6.1 10.6 %copy-start.3 = (bf16[5,2,8,256]{3,2,1,0:T(8,128)(2,1)S(1)}, bf16[5,2,8,256]{3,2,1,0:T(8,128)(2,1)}, u32[]{:S(2)}) copy-start(bf16[5,2,8,256]{3,2,1,0:T(8,128)(2,1)} %rest_4_.1) | copy-start | bytes 122884
  6.1 10.6 %copy-start.4 = (bf16[5,2,8,256]{3,2,1,0:T(8,128)(2,1)S(1)}, bf16[5,2,8,256]{3,2,1,0:T(8,128)(2,1)}, u32[]{:S(2)}) copy-start(bf16[5,2,8,256]{3,2,1,0:T(8,128)(2,1)} %rest_5_.1) | copy-start | bytes 122884
  6.1 10.6 %copy-start.5 = (bf16[5,2,256,8]{2,3,1,0:T(8,128)(2,1)S(1)}, bf16[5,2,256,8]{2,3,1,0:T(8,128)(2,1)}, u32[]{:S(2)}) copy-start(bf16[5,2,256,8]{2,3,1,0:T(8,128)(2,1)} %param.17) | copy-start | bytes 122884
  6.1 10.6 %copy-start.6 = (bf16[5,2,256,8]{2,3,1,0:T(8,128)(2,1)S(1)}, bf16[5,2,256,8]{2,3,1,0:T(8,128)(2,1)}, u32[]{:S(2)}) copy-start(bf16[5,2,256,8]{2,3,1,0:T(8,128)(2,1)} %param.18) | copy-start | bytes 122884
  6.1 6.1 %collective-permute-start.1 = (f32[96,128]{1,0:T(8,128)S(1)}, f32[96,128]{1,0:T(8,128)S(1)}, u32[]{:S(2)}, u32[]{:S(2)}) collective-permute-start(f32[96,128]{1,0:T(8,128)S(1)} %get-tuple-element.8), channel_id=1, source_target_pairs={{2,0},{4,2},{6,4},{3,1},{5,3},{7,5},{10,8},{12,10},{14,12},{11,9},... | collective-permute-start | bytes 147464 | tf_op jit(solution)/shard_map/ppermute | solution.py:290
  12.3 4.5 %copy-start.8 = (f32[4,5,2]{1,2,0:T(2,128)S(1)}, f32[4,5,2]{1,2,0:T(2,128)}, u32[]{:S(2)}) copy-start(f32[4,5,2]{1,2,0:T(2,128)} %param.19) | copy-start | bytes 484
  12.5 4.2 %copy-start.7 = (f32[2,5,5]{2,0,1:T(2,128)S(1)}, f32[2,5,5]{2,0,1:T(2,128)}, u32[]{:S(2)}) copy-start(f32[2,5,5]{2,0,1:T(2,128)} %param.14) | copy-start | bytes 604
  12.5 4.2 %collective-permute-start.2 = (f32[96,128]{1,0:T(8,128)S(1)}, f32[96,128]{1,0:T(8,128)S(1)}, u32[]{:S(2)}, u32[]{:S(2)}) collective-permute-start(f32[96,128]{1,0:T(8,128)S(1)} %pack_x.1), channel_id=1, source_target_pairs={{0,1},{1,0},{2,3},{3,2},{4,5},{5,4},{6,7},{7,6},{8,9},{9,8},{10,11... | collective-permute-start | bytes 147464 | tf_op jit(solution)/shard_map/ppermute | solution.py:305
  16.7 0.7 %copy-start.9 = (f32[2]{0:T(128)S(1)}, f32[2]{0:T(128)}, u32[]{:S(2)}) copy-start(f32[2]{0:T(128)} %rest_1_.1) | copy-start | bytes 28
  16.7 0.7 %copy-start.10 = (f32[2]{0:T(128)S(1)}, f32[2]{0:T(128)}, u32[]{:S(2)}) copy-start(f32[2]{0:T(128)} %rest_2_.1) | copy-start | bytes 28
  16.7 0.7 %copy-start.11 = (s32[4]{0:T(128)S(1)}, s32[4]{0:T(128)}, u32[]{:S(2)}) copy-start(s32[4]{0:T(128)} %rest_9_.1) | copy-start | bytes 52

commit v3 on v0

v3 whole, which is shorter than its diff:
```python
import functools

import jax
import jax.numpy as jnp
import numpy as np
from jax import lax
from jax.experimental import pallas as pl
from jax.experimental.pallas import tpu as pltpu
from jax.sharding import PartitionSpec as P

RELAX = 0.25
REACH = 3
HALO = 3 * REACH
PAD = 16
LANES = 128
FIRST = PAD - 8
THIRD, HALF = 1.0 / 3.0, 0.5

UPWIND = (-2.0, 15.0, -60.0, 20.0, 30.0, -3.0, 0.0)
CENTRAL = (-1.0, 9.0, -45.0, 0.0, 45.0, -9.0, 1.0)
DAMPING = (1.0, -6.0, 15.0, -20.0, 15.0, -6.0, 1.0)


def lane_of(col, cols):
    if col < 0:
        return 2 * LANES + col
    return col if col < cols else LANES + col - cols


def band_matrices(cols):
    bands = np.zeros((2, 2 * LANES, 2 * LANES), np.float32)
    for col in range(-HALO, cols + HALO):
        for offset in range(-REACH, REACH + 1):
            if -HALO <= col + offset < cols + HALO:
                at = lane_of(col + offset, cols), lane_of(col, cols)
                bands[0][at] = UPWIND[offset + REACH]
                bands[1][at] = -UPWIND[REACH - offset]
    return bands


def iota(shape, dim):
    return lax.broadcasted_iota(jnp.int32, shape, dim)


def edge_weight(distance, width):
    dist = distance.astype(jnp.float32)
    inside = (dist >= 0.0) & (dist < width)
    return jnp.where(inside, jnp.square((width - dist) / width), 0.0)


def slots(count_f, count_l):
    return [(f, l, HALO * (f * count_l + l)) for f in range(count_f) for l in range(count_l)]


def pack_y_kernel(fields, first_round, second_round):
    count_f, count_l, rows, _ = fields.shape
    even = lax.rem(lax.axis_index("gy"), 2) == 0
    for f, l, slot in slots(count_f, count_l):
        top = fields[f, l, 0:HALO, :]
        bottom = fields[f, l, rows - HALO : rows, :]
        first_round[slot : slot + HALO, :] = jnp.where(even, bottom, top)
        second_round[slot : slot + HALO, :] = jnp.where(even, top, bottom)


def halo_rows(gy_count, first_round, second_round, slot):
    gy = lax.axis_index("gy")
    even = lax.rem(gy, 2) == 0
    first = first_round[slot : slot + HALO, :]
    second = second_round[slot : slot + HALO, :]
    north = jnp.where(gy == 0, 0.0, jnp.where(even, second, first))
    south = jnp.where(gy == gy_count - 1, 0.0, jnp.where(even, first, second))
    return north, south


def sent_starts(gx_count, cols):
    if gx_count == 2:
        return [jnp.where(lax.axis_index("gx") == 0, cols - HALO, 0)]
    return [cols - HALO, 0]


def prepare_kernel(
    grid_sizes, fields, north, south, west, east, scale, widths, drive, relax, inside, *rest
):
    gy_count, gx_count = grid_sizes
    payloads, wide = rest[:-1], rest[-1]
    count_f, count_l, rows, cols = fields.shape
    ext_rows = relax.shape[1]
    strip = north.shape[2]
    total_rows, total_cols = rows * gy_count, cols * gx_count
    gy, gx = lax.axis_index("gy"), lax.axis_index("gx")
    row_start, col_start = gy * rows, gx * cols
    width = [widths[s].astype(jnp.float32) for s in range(4)]

    lane_rows = iota((rows, LANES), 1)
    starts = sent_starts(gx_count, cols)
    packed = [jnp.zeros((rows, LANES), jnp.float32) for _ in starts]
    if cols < LANES:
        wide[...] = jnp.zeros_like(wide)
    for f, l, slot in slots(count_f, count_l):
        if cols < LANES:
            wide[:, 0:cols] = fields[f, l]
            own = wide[...]
        else:
            own = fields[f, l]
        for n, start in enumerate(starts):
            moved = pltpu.roll(own, lax.rem(slot + LANES - start, LANES), 1)
            here = (lane_rows >= slot) & (lane_rows < slot + HALO)
            packed[n] = jnp.where(here, moved, packed[n])
    for payload, value in zip(payloads, packed):
        payload[...] = value

    lane = iota((ext_rows, LANES), 1)
    row_global = iota((ext_rows, LANES), 0) + (row_start - PAD)
    row_weight = edge_weight(row_global, width[0]) + edge_weight(
        total_rows - 1 - row_global, width[1]
    )
    lane_one = iota((8, LANES), 1)
    outer_lane = jnp.where(lane_one >= LANES - HALO, lane_one - LANES, lane_one + cols)
    for t, col in enumerate((lane_one, outer_lane)):
        col_weight = edge_weight(col + col_start, width[2]) + edge_weight(
            total_cols - 1 - (col + col_start), width[3]
        )
        relax[t] = RELAX * (row_weight + col_weight[0:1, :])
    outer_col = jnp.where(lane >= LANES - HALO, lane - LANES, lane + cols) + col_start
    inside[...] = jnp.where(
        (row_global >= 0)
        & (row_global < total_rows)
        & (outer_col >= 0)
        & (outer_col < total_cols),
        1.0,
        0.0,
    )

    pos = iota((strip, LANES), 1)
    depth = iota((strip, LANES), 0)
    pick = jnp.concatenate([pos == depth, pos == depth + (cols - strip)], axis=0)
    pick = pick.astype(jnp.float32).astype(jnp.bfloat16)
    west_weight = RELAX * edge_weight(lane_one + col_start, width[2])
    east_weight = RELAX * edge_weight(total_cols - 1 - (lane_one + col_start), width[3])
    west_weight = jnp.where(lane_one < strip, west_weight, 0.0)
    east_weight = jnp.where((lane_one >= cols - strip) & (lane_one < cols), east_weight, 0.0)
    shift = lax.rem(PAD + total_rows - row_start, total_rows)
    for f in range(count_f):
        for l in range(count_l):
            both = jnp.concatenate([west[f, l], east[f, l]], axis=0).astype(jnp.float32)
            both = pltpu.roll(both, shift, 1)[:, 0:LANES].astype(jnp.bfloat16)
            raw = lax.dot_general(
                both, pick, (((0,), (0,)), ((), ())), preferred_element_type=jnp.float32
            )
            factor = west_weight * scale[2, l, f] + east_weight * scale[3, l, f]
            drive[0, f, l] = raw[0:ext_rows] * factor[0:1, :]
    drive[1] = jnp.zeros(drive.shape[1:], jnp.float32)

    own_shift = lax.rem(total_cols - col_start, total_cols)
    outer_shift = lax.rem(2 * total_cols - cols - col_start, total_cols)
    for source, side, at, here in (
        (north, 0, PAD, gy == 0),
        (south, 1, PAD + rows - strip, gy == gy_count - 1),
    ):

        @pl.when(here)
        def _(source=source, side=side, at=at):
            distance = depth if side == 0 else strip - 1 - depth
            weight = RELAX * edge_weight(distance, width[side])
            for f in range(count_f):
                for l in range(count_l):
                    values = source[f, l].astype(jnp.float32)
                    own = pltpu.roll(values, own_shift, 1)
                    outer = pltpu.roll(values, outer_shift, 1)[:, 0:LANES]
                    outer = jnp.where(
                        pos >= LANES - HALO, own[:, total_cols - LANES : total_cols], outer
                    )
                    factor = weight * scale[side, l, f]
                    old = drive[0, f, l, at : at + strip, :]
                    drive[0, f, l, at : at + strip, :] = old + factor * own[:, 0:LANES]
                    drive[1, f, l, at : at + strip, :] = factor * outer


def pack_x_kernel(grid_sizes, first_round, second_round, *rest):
    gy_count, gx_count = grid_sizes
    sides = (len(rest) - 1) // 2
    payloads, outs, ext = rest[:sides], rest[sides:-1], rest[-1]
    cols = first_round.shape[1]
    rows = payloads[0].shape[0]
    lane = iota((2 * PAD, LANES), 1)
    starts = sent_starts(gx_count, cols)
    packed = [jnp.zeros((2 * PAD, LANES), jnp.float32) for _ in starts]
    ext[...] = jnp.zeros_like(ext)
    for index in range(ext.shape[0]):
        slot = index * HALO
        north, south = halo_rows(gy_count, first_round, second_round, slot)
        ext[index, PAD - HALO : PAD, 0:cols] = north
        ext[index, PAD : PAD + HALO, 0:cols] = south
        for n, start in enumerate(starts):
            moved = pltpu.roll(ext[index], lax.rem(slot + LANES - start, LANES), 1)
            packed[n] = jnp.where((lane >= slot) & (lane < slot + HALO), moved, packed[n])
    for out, payload, value in zip(outs, payloads, packed):
        out[0:PAD, :] = value[0:PAD]
        out[PAD : PAD + rows, :] = payload[...]
        out[PAD + rows : 2 * PAD + rows, :] = value[PAD : 2 * PAD]


def level_weights(coupling, wind_y, l, fac, count_f):
    scaled, scaled_abs = fac / 60.0 * wind_y[l], fac / 60.0 * jnp.abs(wind_y[l])
    taps = [scaled_abs * DAMPING[k] - scaled * CENTRAL[k] for k in range(2 * REACH + 1)]
    mix = [
        [fac * coupling[f, l, g] + (taps[REACH] if f == g else 0.0) for g in range(count_f)]
        for f in range(count_f)
    ]
    return taps, mix


def cell_terms(src, l, f, at, centers, weight, taps, mix, total):
    for g, center in enumerate(centers):
        total = total + (mix[f][g] - weight if g == f else mix[f][g]) * center
    for k in range(2 * REACH + 1):
        if k != REACH:
            total = total + taps[k] * src[f, l, pl.ds(at + (k - REACH), 8), :]
    return total


def begin_kernel(
    gy_count,
    fields,
    first_round,
    second_round,
    drive,
    relax,
    wind_y,
    coupling,
    state,
    part_one,
    base_two,
    base_three,
):
    count_f, count_l, rows, cols = fields.shape
    ext_rows = state.shape[2]
    state[...] = jnp.zeros_like(state)
    for f, l, slot in slots(count_f, count_l):
        north, south = halo_rows(gy_count, first_round, second_round, slot)
        state[f, l, PAD - HALO : PAD, 0:cols] = north
        state[f, l, PAD : PAD + rows, 0:cols] = fields[f, l]
        state[f, l, PAD + rows : PAD + rows + HALO, 0:cols] = south
    for l in range(count_l):
        taps, mix = level_weights(coupling, wind_y, l, THIRD, count_f)

        def group(n, _):
            at = pl.multiple_of(FIRST + n * 8, 8)
            to = pl.multiple_of(n * 8, 8)
            centers = [state[g, l, pl.ds(at, 8), :] for g in range(count_f)]
            weight = THIRD * relax[0, pl.ds(at, 8), :]
            for f in range(count_f):
                forced = drive[0, f, l, pl.ds(at, 8), :]
                base_two[f, l, pl.ds(to, 8), :] = centers[f] + HALF * forced
                base_three[f, l, pl.ds(to, 8), :] = centers[f] + forced
                total = centers[f] + THIRD * forced
                total = cell_terms(state, l, f, at, centers, weight, taps, mix, total)
                part_one[f, l, pl.ds(to, 8), :] = total
            return 0

        lax.fori_loop(0, (rows + 16) // 8, group, 0)


def finish_kernel(grid_sizes, sides, *refs):
    gy_count, gx_count = grid_sizes
    side = refs[:sides]
    (
        state,
        part_one,
        base_two,
        base_three,
        drive,
        relax,
        inside,
        wind_x,
        wind_y,
        coupling,
        bands,
        out,
        outer,
        own_one,
        outer_one,
        own_two,
        outer_two,
        xdiv,
    ) = refs[sides:]
    count_f, count_l, rows, cols = out.shape
    ext_rows = state.shape[2]
    gy, gx = lax.axis_index("gy"), lax.axis_index("gx")

    lane = iota((ext_rows, LANES), 1)
    for f, l, slot in slots(count_f, count_l):
        if sides == 1:
            placed = [(side[0], jnp.where(gx == 0, 0, LANES - HALO))]
        else:
            placed = [(side[0], LANES - HALO), (side[1], 0)]
        merged = jnp.zeros((ext_rows, LANES), jnp.float32)
        for source, target in placed:
            moved = pltpu.roll(source[...], lax.rem(target + LANES - slot, LANES), 1)
            merged = jnp.where((lane >= target) & (lane < target + HALO), moved, merged)
        outer[f, l] = merged

    def x_divergence(own, outer_cols, l, first, height, tiles):
        flat = [
            source[:, l, first : first + height, :].reshape(count_f * height, LANES)
            for source in (own, outer_cols)
        ]
        whole = jnp.concatenate(flat, axis=1)
        high = whole.astype(jnp.bfloat16)
        low = (whole - high.astype(jnp.float32)).astype(jnp.bfloat16)
        band = bands[jnp.where(wind_x[l] < 0.0, 1, 0)][:, 0 : tiles * LANES]
        moved = jnp.dot(high, band, preferred_element_type=jnp.float32) + jnp.dot(
            low, band, preferred_element_type=jnp.float32
        )
        for t in range(tiles):
            xdiv[t, :, 0:height, :] = moved[:, t * LANES : (t + 1) * LANES].reshape(
                count_f, height, LANES
            )

    def outside_rows(dst):
        @pl.when(gy == 0)
        def _():
            dst[:, :, FIRST : FIRST + 8, :] = jnp.zeros((count_f, count_l, 8, LANES), jnp.float32)

        @pl.when(gy == gy_count - 1)
        def _():
            dst[:, :, PAD + rows : PAD + rows + 8, :] = jnp.zeros(
                (count_f, count_l, 8, LANES), jnp.float32
            )

    groups = (rows + 16) // 8
    for own, outer_cols, own_next, outer_next, fac in (
        (state, outer, own_one, outer_one, THIRD),
        (own_one, outer_one, own_two, outer_two, HALF),
    ):
        for l in range(count_l):
            x_divergence(own, outer_cols, l, FIRST, groups * 8, 2)
            taps, mix = level_weights(coupling, wind_y, l, fac, count_f)
            scaled_x = fac / 60.0 * wind_x[l]

            def group(n, _):
                at = pl.multiple_of(FIRST + n * 8, 8)
                to = pl.multiple_of(n * 8, 8)
                centers = [outer_cols[g, l, pl.ds(at, 8), :] for g in range(count_f)]
                weight = fac * relax[1, pl.ds(at, 8), :]
                kept = inside[pl.ds(at, 8), :]
                for f in range(count_f):
                    total = outer[f, l, pl.ds(at, 8), :] + fac * drive[1, f, l, pl.ds(at, 8), :]
                    total = total - scaled_x * xdiv[1, f, pl.ds(to, 8), :]
                    total = cell_terms(outer_cols, l, f, at, centers, weight, taps, mix, total)
                    outer_next[f, l, pl.ds(at, 8), :] = total * kept
                if own is state:
                    for f in range(count_f):
                        total = part_one[f, l, pl.ds(to, 8), :]
                        own_next[f, l, pl.ds(at, 8), :] = (
                            total - scaled_x * xdiv[0, f, pl.ds(to, 8), :]
                        )
                else:
                    centers = [own[g, l, pl.ds(at, 8), :] for g in range(count_f)]
                    weight = fac * relax[0, pl.ds(at, 8), :]
                    for f in range(count_f):
                        total = base_two[f, l, pl.ds(to, 8), :]
                        total = total - scaled_x * xdiv[0, f, pl.ds(to, 8), :]
                        own_next[f, l, pl.ds(at, 8), :] = cell_terms(
                            own, l, f, at, centers, weight, taps, mix, total
                        )
                return 0

            lax.fori_loop(0, groups, group, 0)
        outside_rows(own_next)

    for l in range(count_l):
        x_divergence(own_two, outer_two, l, PAD, rows, 1)
        taps, mix = level_weights(coupling, wind_y, l, 1.0, count_f)
        scaled_x = wind_x[l] / 60.0

        def group(n, _):
            at = pl.multiple_of(PAD + n * 8, 8)
            to = pl.multiple_of(n * 8, 8)
            centers = [own_two[g, l, pl.ds(at, 8), :] for g in range(count_f)]
            weight = relax[0, pl.ds(at, 8), :]
            for f in range(count_f):
                total = base_three[f, l, pl.ds(to + 8, 8), :]
                total = total - scaled_x * xdiv[0, f, pl.ds(to, 8), :]
                total = cell_terms(own_two, l, f, at, centers, weight, taps, mix, total)
                out[f, l, pl.ds(to, 8), :] = total[:, 0:cols]
            return 0

        lax.fori_loop(0, rows // 8, group, 0)


def pair_rounds(gy_count, gx_count):
    rounds = []
    for start in (0, 1):
        partner = {}
        for low in range(start, gy_count - 1, 2):
            partner[low], partner[low + 1] = low + 1, low
        pairs = []
        for y in range(gy_count):
            for x in range(gx_count):
                if y in partner:
                    pairs.append((y * gx_count + x, partner[y] * gx_count + x))
                elif gx_count % 2 == 0:
                    pairs.append((y * gx_count + x, y * gx_count + (x ^ 1)))
        rounds.append(pairs)
    return rounds


def local(
    gy_count, gx_count, fields, wind_x, wind_y, coupling, north, south, west, east, strip_scale, widths
):
    count_f, count_l, rows, cols = fields.shape
    ext_rows = rows + 2 * PAD
    grid_sizes = (gy_count, gx_count)
    packed_rows = -(-HALO * count_f * count_l // 8) * 8
    vmem = pl.BlockSpec(memory_space=pltpu.VMEM)
    smem = pl.BlockSpec(memory_space=pltpu.SMEM)
    f32 = functools.partial(jax.ShapeDtypeStruct, dtype=jnp.float32)

    def call(body, name, out_shape, inputs, scratch=(), limit=4):
        several = isinstance(out_shape, tuple)
        return pl.pallas_call(
            body,
            out_shape=out_shape,
            in_specs=[space for _, space in inputs],
            out_specs=(vmem,) * len(out_shape) if several else vmem,
            scratch_shapes=list(scratch),
            compiler_params=pltpu.CompilerParams(vmem_limit_bytes=limit << 20),
            name=name,
        )(*[value for value, _ in inputs])

    def inputs(space, *values):
        return [(value, space) for value in values]

    strip_shape = f32((packed_rows, cols))
    sent_first, sent_second = call(
        pack_y_kernel, "pack_y", (strip_shape, strip_shape), inputs(vmem, fields)
    )
    first_pairs, second_pairs = pair_rounds(gy_count, gx_count)
    first_round = lax.ppermute(sent_first, ("gy", "gx"), first_pairs)
    second_round = lax.ppermute(sent_second, ("gy", "gx"), second_pairs)

    mixing = jnp.transpose(coupling, (1, 0, 2))
    scales = jnp.transpose(strip_scale, (0, 2, 1))
    sides = 1 if gx_count == 2 else 2
    state_shape = (count_f, count_l, ext_rows, LANES)
    prepared = call(
        functools.partial(prepare_kernel, grid_sizes),
        "prepare",
        (f32((2,) + state_shape), f32((2, ext_rows, LANES)), f32((ext_rows, LANES)))
        + (f32((rows, LANES)),) * sides,
        inputs(vmem, fields, north, south, jnp.swapaxes(west, 2, 3), jnp.swapaxes(east, 2, 3))
        + inputs(smem, scales, widths),
        scratch=[pltpu.VMEM((rows, LANES), jnp.float32)],
    )
    drive, relax, inside = prepared[:3]

    sent = call(
        functools.partial(pack_x_kernel, grid_sizes),
        "pack_x",
        (f32((ext_rows, LANES)),) * sides,
        inputs(vmem, first_round, second_round, *prepared[3:]),
        scratch=[pltpu.VMEM((count_f * count_l, 2 * PAD, LANES), jnp.float32)],
    )
    forward = [(i, i + 1) for i in range(gx_count - 1)]
    backward = [(b, a) for a, b in forward]
    if sides == 1:
        side = [lax.ppermute(sent[0], "gx", forward + backward)]
    else:
        side = [lax.ppermute(sent[0], "gx", forward), lax.ppermute(sent[1], "gx", backward)]

    wide_shape = (count_f, count_l, rows + 16, LANES)
    begun = call(
        functools.partial(begin_kernel, gy_count),
        "begin",
        (f32(state_shape), f32(wide_shape), f32(wide_shape), f32(wide_shape)),
        inputs(vmem, fields, first_round, second_round, drive, relax)
        + inputs(smem, wind_y, mixing),
    )
    bands = jnp.asarray(band_matrices(cols), jnp.bfloat16)
    return call(
        functools.partial(finish_kernel, grid_sizes, sides),
        "finish",
        f32(fields.shape),
        inputs(vmem, *side, *begun, drive, relax, inside)
        + inputs(smem, wind_x, wind_y, mixing)
        + inputs(vmem, bands),
        scratch=[pltpu.VMEM(state_shape, jnp.float32)] * 5
        + [pltpu.VMEM((2, count_f, rows + 16, LANES), jnp.float32)],
        limit=12,
    )


def solution(mesh):
    return jax.shard_map(
        functools.partial(local, mesh.shape["gy"], mesh.shape["gx"]),
        mesh=mesh,
        in_specs=(
            P("mem", None, "gy", "gx"),
            P("mem"),
            P("mem"),
            P(),
            P("mem", None, None, None),
            P("mem", None, None, None),
            P("mem", None, None, None),
            P("mem", None, None, None),
            P("mem", None, None),
            P(),
        ),
        out_specs=P("mem", None, "gy", "gx"),
        check_vma=False,
    )
```

time: 83.3 us -> 19.3 us (0.23)
  starting transfers between devices: 34.5 us -> 6.16 us
  local copies, waits for them, and re-layouts: 23.7 us -> 2.93 us
  other arithmetic: 10.6 us -> 0 us
  waiting for transfers between devices: 10.2 us -> 1.26 us
  Pallas kernels: 0 us -> 8.67 us
  matrix products: 2.97 us -> 0 us
    ppermute x12 -> x3, starting transfers between devices: 34.5 us -> 6.16 us  [the longest x1 3.12 us: local(): first_round = lax.ppermute(sent_first, ('gy', 'gx'), first_pairs)]
    gather x12 -> x0, local copies, waits for them, and re-layouts: 12 us -> none  [strip_values(): picked = jnp.take(jnp.take(strip, rows, axis=2), cols, axis=3)]
    ppermute x12 -> x3, waiting for transfers between devices: 10.2 us -> 1.26 us  [the longest x1 0.77 us: local(): second_round = lax.ppermute(sent_second, ('gy', 'gx'), second_pairs)]
    pallas_call x0 -> x5, Pallas kernels: none -> 8.67 us  [call(): pl.pallas_call(body, out_shape=out_shape, in_specs=[space for _, space in...]
    div x6 -> x0, other arithmetic: 6.05 us -> none  [divergence(): flux = (wind * centered - jnp.abs(wind) * damping) / 60.0]
    slice x13 -> x0, local copies, waits for them, and re-layouts: 5.13 us -> none  [the longest x6 2.9 us: extended(): lax.slice_in_dim(block, 0, width, axis=dim)]
    dot_general x3 -> x0, matrix products: 2.97 us -> none  [tendency(): jnp.einsum('lfg,glyx->flyx', coupling, center, precision=lax.Precision.HI...]
    select_n x9 -> x0, other arithmetic: 1.84 us -> none  [the longest x1 1.22 us: profile(): jnp.where((dist_float >= 0.0) & (dist_float < width), jnp.square((width -...]
  transfers between devices with their start and end apart: 12 -> 3, of which waited for: 6 -> 2; matrix products, arithmetic and copies ran while one was open for 28% -> 0% of each run, Pallas kernels for 0% -> 14%
where the time goes in v3:
time: 19.3 us; the launch traced here: 19.1 us
  Pallas kernels  8.67 us (45%)
  starting transfers between devices  6.16 us (32%)
  local copies, waits for them, and re-layouts  2.93 us (15%)
  waiting for transfers between devices  1.26 us (7%)
    pallas_call x5, Pallas kernels, call(): pl.pallas_call(body, out_shape=out_shape, in_specs=[space for _, space in...  8.67 us
    ppermute x1, starting transfers between devices, local(): first_round = lax.ppermute(sent_first, ('gy', 'gx'), first_pairs)  3.12 us
    unnamed x24, local copies, waits for them, and re-layouts  2.93 us
    ppermute x1, starting transfers between devices, local(): side = [lax.ppermute(sent[0], 'gx', forward + backward)]  1.56 us
    ppermute x1, starting transfers between devices, local(): second_round = lax.ppermute(sent_second, ('gy', 'gx'), second_pairs)  1.49 us
    ppermute x1, waiting for transfers between devices, local(): second_round = lax.ppermute(sent_second, ('gy', 'gx'), second_pairs)  0.77 us
    ppermute x1, waiting for transfers between devices, local(): side = [lax.ppermute(sent[0], 'gx', forward + backward)]  0.48 us
  transfers between devices with their start and end apart: 3, of which 2 were waited for; matrix products, arithmetic and copies ran while one was open for 0% of the time, Pallas kernels for 14%

profile of v3, /device:TPU:0, one launch (start us, length us, event | category | flops | bytes accessed | tf_op | source)
XLA Modules:
  0.0 19.1 jit_solution(4213178220707714867)
XLA Ops:
  0.0 0.0 copy-start
  0.0 1.0 %copy-done = f32[5,2,64,128]{3,2,1,0:T(8,128)S(1)} copy-done((f32[5,2,64,128]{3,2,1,0:T(8,128)S(1)}, f32[5,2,64,128]{3,2,1,0:T(8,128)}, u32[]{:S(2)}) %copy-start) | copy-done | bytes 327704
  1.0 0.0 copy-start.3
  1.0 0.0 copy-start.4
  1.0 0.0 copy-start.5
  1.0 0.0 copy-start.6
  1.0 0.0 copy-start.8
  1.0 3.1 %collective-permute-start = (f32[96,128]{1,0:T(8,128)S(1)}, f32[96,128]{1,0:T(8,128)S(1)}, u32[]{:S(2)}, u32[]{:S(2)}) collective-permute-start(f32[96,128]{1,0:T(8,128)S(1)} %get-tuple-element.15), channel_id=1, source_target_pairs={{0,2},{1,3},{2,0},{3,1},{4,6},{5,7},{6,4},{7,5},{8,10},{9,11},{10,... | collective-permute-start | bytes 147464 | tf_op jit(solution)/shard_map/ppermute | solution.py:440
  4.2 1.5 %collective-permute-start.1 = (f32[96,128]{1,0:T(8,128)S(1)}, f32[96,128]{1,0:T(8,128)S(1)}, u32[]{:S(2)}, u32[]{:S(2)}) collective-permute-start(f32[96,128]{1,0:T(8,128)S(1)} %get-tuple-element.16), channel_id=1, source_target_pairs={{0,1},{1,0},{2,4},{3,5},{4,2},{5,3},{6,7},{7,6},{8,9},{9,8},{10,12... | collective-permute-start | bytes 147464 | tf_op jit(solution)/shard_map/ppermute | solution.py:441
  5.6 0.0 copy-start.10
  5.6 0.0 copy-done.3
  5.6 0.0 copy-done.4
  5.6 0.0 copy-done.5
  5.7 0.0 copy-done.6
  5.7 0.0 copy-done.8
  5.7 0.6 %copy-done.10 = s32[4]{0:T(128)S(1)} copy-done((s32[4]{0:T(128)S(1)}, s32[4]{0:T(128)}, u32[]{:S(2)}) %copy-start.10) | copy-done | bytes 40
  6.3 0.0 copy-start.1
  6.3 1.1 %prepare.1 = (f32[2,5,2,96,128]{4,3,2,1,0:T(8,128)S(1)}, f32[2,96,128]{2,1,0:T(8,128)S(1)}, f32[96,128]{1,0:T(8,128)S(1)}, f32[64,128]{1,0:T(8,128)S(1)}) custom-call(f32[5,2,64,128]{3,2,1,0:T(8,128)S(1)} %copy-done, bf16[5,2,8,256]{3,2,1,0:T(8,128)(2,1)S(1)} %copy-done.3, bf16[5,2,8,256]{3,2,1,0:T(8,128)(2,1)S(1)} %copy-done.4, ...), custom_call_target="tpu_custom_call" | custom-call | tf_op jit(solution)/shard_map/prepare/pallas_call | solution.py:422
  7.5 0.0 collective-permute-done.first_round
  7.5 0.8 %collective-permute-done.1.second_round = f32[96,128]{1,0:T(8,128)S(1)} collective-permute-done((f32[96,128]{1,0:T(8,128)S(1)}, f32[96,128]{1,0:T(8,128)S(1)}, u32[]{:S(2)}, u32[]{:S(2)}) %collective-permute-start.1) | collective-permute-done | bytes 49184 | tf_op jit(solution)/shard_map/ppermute | solution.py:441
  8.2 0.1 pack_x.1
  8.4 0.0 copy-start.7
  8.4 1.6 %collective-permute-start.2 = (f32[96,128]{1,0:T(8,128)S(1)}, f32[96,128]{1,0:T(8,128)S(1)}, u32[]{:S(2)}, u32[]{:S(2)}) collective-permute-start(f32[96,128]{1,0:T(8,128)S(1)} %pack_x.1), channel_id=1, source_target_pairs={{0,1},{1,0},{2,3},{3,2},{4,5},{5,4},{6,7},{7,6},{8,9},{9,8},{10,11... | collective-permute-start | bytes 147464 | tf_op jit(solution)/shard_map/ppermute | solution.py:468
  9.9 0.0 copy-start.9
  9.9 0.0 copy-done.1
  9.9 0.0 copy-done.7
  9.9 0.6 %copy-done.9 = f32[2]{0:T(128)S(1)} copy-done((f32[2]{0:T(128)S(1)}, f32[2]{0:T(128)}, u32[]{:S(2)}) %copy-start.9) | copy-done | bytes 32
  10.6 1.5 %begin.1 = (f32[5,2,96,128]{3,2,1,0:T(8,128)S(1)}, f32[5,2,80,128]{3,2,1,0:T(8,128)S(1)}, f32[5,2,80,128]{3,2,1,0:T(8,128)S(1)}, f32[5,2,80,128]{3,2,1,0:T(8,128)S(1)}) custom-call(f32[5,2,64,128]{3,2,1,0:T(8,128)S(1)} %copy-done.1, f32[96,128]{1,0:T(8,128)S(1)} %collective-permute-done.first_round, f32[96,128]{1,0:T(8,128)S(1)} %collective-permute-done.1.second_round, ...), custom_call_target="tpu_custom_call" | custom-call | tf_op jit(solution)/shard_map/begin/pallas_call | solution.py:422
  12.1 0.5 %collective-permute-done.2.refs_0_ = f32[96,128]{1,0:T(8,128)S(1)} collective-permute-done((f32[96,128]{1,0:T(8,128)S(1)}, f32[96,128]{1,0:T(8,128)S(1)}, u32[]{:S(2)}, u32[]{:S(2)}) %collective-permute-start.2) | collective-permute-done | bytes 49184 | tf_op jit(solution)/shard_map/ppermute | solution.py:468
  12.5 0.0 copy-done.2
  12.5 0.7 %copy-done.11 = f32[2]{0:T(128)S(1)} copy-done((f32[2]{0:T(128)S(1)}, f32[2]{0:T(128)}, u32[]{:S(2)}) %copy-start.11) | copy-done | bytes 32
  13.2 5.9 %finish.1 = f32[5,2,64,128]{3,2,1,0:T(8,128)} custom-call(f32[96,128]{1,0:T(8,128)S(1)} %collective-permute-done.2.refs_0_, f32[5,2,96,128]{3,2,1,0:T(8,128)S(1)} %get-tuple-element.20.refs_1_, f32[5,2,80,128]{3,2,1,0:T(8,128)S(1)} %get-tuple-element.21.refs_2_, f32[5,2,80,128]{3,2,1,0:T(8,128)S(1)} %get-tuple-element.22.refs_3_, ...), custom_call_target="tpu_custom_call" | custom-call | tf_op jit(solution)/shard_map/finish/pallas_call | solution.py:422
  (3 shorter events, 0.0 us)
Async XLA Ops:
  0.0 1.0 %copy-start = (f32[5,2,64,128]{3,2,1,0:T(8,128)S(1)}, f32[5,2,64,128]{3,2,1,0:T(8,128)}, u32[]{:S(2)}) copy-start(f32[5,2,64,128]{3,2,1,0:T(8,128)} %fields.5) | copy-start | bytes 983044
  1.0 4.7 %copy-start.3 = (bf16[5,2,8,256]{3,2,1,0:T(8,128)(2,1)S(1)}, bf16[5,2,8,256]{3,2,1,0:T(8,128)(2,1)}, u32[]{:S(2)}) copy-start(bf16[5,2,8,256]{3,2,1,0:T(8,128)(2,1)} %north.1) | copy-start | bytes 122884
  1.0 4.7 %copy-start.4 = (bf16[5,2,8,256]{3,2,1,0:T(8,128)(2,1)S(1)}, bf16[5,2,8,256]{3,2,1,0:T(8,128)(2,1)}, u32[]{:S(2)}) copy-start(bf16[5,2,8,256]{3,2,1,0:T(8,128)(2,1)} %south.1) | copy-start | bytes 122884
  1.0 4.7 %copy-start.5 = (bf16[5,2,256,8]{2,3,1,0:T(8,128)(2,1)S(1)}, bf16[5,2,256,8]{2,3,1,0:T(8,128)(2,1)}, u32[]{:S(2)}) copy-start(bf16[5,2,256,8]{2,3,1,0:T(8,128)(2,1)} %param.17) | copy-start | bytes 122884
  1.0 4.7 %copy-start.6 = (bf16[5,2,256,8]{2,3,1,0:T(8,128)(2,1)S(1)}, bf16[5,2,256,8]{2,3,1,0:T(8,128)(2,1)}, u32[]{:S(2)}) copy-start(bf16[5,2,256,8]{2,3,1,0:T(8,128)(2,1)} %param.18) | copy-start | bytes 122884
  1.0 4.6 %copy-start.8 = (f32[4,5,2]{1,2,0:T(2,128)S(1)}, f32[4,5,2]{1,2,0:T(2,128)}, u32[]{:S(2)}) copy-start(f32[4,5,2]{1,2,0:T(2,128)} %param.19) | copy-start | bytes 484
  1.0 6.4 %collective-permute-start = (f32[96,128]{1,0:T(8,128)S(1)}, f32[96,128]{1,0:T(8,128)S(1)}, u32[]{:S(2)}, u32[]{:S(2)}) collective-permute-start(f32[96,128]{1,0:T(8,128)S(1)} %get-tuple-element.15), channel_id=1, source_target_pairs={{0,2},{1,3},{2,0},{3,1},{4,6},{5,7},{6,4},{7,5},{8,10},{9,11},{10,... | collective-permute-start | bytes 147464 | tf_op jit(solution)/shard_map/ppermute | solution.py:440
  4.2 4.1 %collective-permute-start.1 = (f32[96,128]{1,0:T(8,128)S(1)}, f32[96,128]{1,0:T(8,128)S(1)}, u32[]{:S(2)}, u32[]{:S(2)}) collective-permute-start(f32[96,128]{1,0:T(8,128)S(1)} %get-tuple-element.16), channel_id=1, source_target_pairs={{0,1},{1,0},{2,4},{3,5},{4,2},{5,3},{6,7},{7,6},{8,9},{9,8},{10,12... | collective-permute-start | bytes 147464 | tf_op jit(solution)/shard_map/ppermute | solution.py:441
  5.6 0.7 %copy-start.10 = (s32[4]{0:T(128)S(1)}, s32[4]{0:T(128)}, u32[]{:S(2)}) copy-start(s32[4]{0:T(128)} %widths.1) | copy-start | bytes 52
  6.3 3.6 %copy-start.1 = (f32[5,2,64,128]{3,2,1,0:T(8,128)S(1)}, f32[5,2,64,128]{3,2,1,0:T(8,128)}, u32[]{:S(2)}) copy-start(f32[5,2,64,128]{3,2,1,0:T(8,128)} %fields.5) | copy-start | bytes 983044
  8.4 1.6 %copy-start.7 = (f32[2,5,5]{2,0,1:T(2,128)S(1)}, f32[2,5,5]{2,0,1:T(2,128)}, u32[]{:S(2)}) copy-start(f32[2,5,5]{2,0,1:T(2,128)} %param.14) | copy-start | bytes 604
  8.4 4.2 %collective-permute-start.2 = (f32[96,128]{1,0:T(8,128)S(1)}, f32[96,128]{1,0:T(8,128)S(1)}, u32[]{:S(2)}, u32[]{:S(2)}) collective-permute-start(f32[96,128]{1,0:T(8,128)S(1)} %pack_x.1), channel_id=1, source_target_pairs={{0,1},{1,0},{2,3},{3,2},{4,5},{5,4},{6,7},{7,6},{8,9},{9,8},{10,11... | collective-permute-start | bytes 147464 | tf_op jit(solution)/shard_map/ppermute | solution.py:468
  9.9 0.7 %copy-start.9 = (f32[2]{0:T(128)S(1)}, f32[2]{0:T(128)}, u32[]{:S(2)}) copy-start(f32[2]{0:T(128)} %refs_9_.1) | copy-start | bytes 28
  10.6 1.9 %copy-start.2 = (bf16[2,256,256]{2,1,0:T(8,128)(2,1)S(1)}, bf16[2,256,256]{2,1,0:T(8,128)(2,1)}, u32[]{:S(2)}) copy-start(bf16[2,256,256]{2,1,0:T(8,128)(2,1)} %constant.2.clone.refs_11_) | copy-start | bytes 786436
  12.5 0.7 %copy-start.11 = (f32[2]{0:T(128)S(1)}, f32[2]{0:T(128)}, u32[]{:S(2)}) copy-start(f32[2]{0:T(128)} %refs_8_.1) | copy-start | bytes 28

commit v4 on v3

v4 whole, which is shorter than its diff:
```python
import functools

import jax
import jax.numpy as jnp
import numpy as np
from jax import lax
from jax.experimental import pallas as pl
from jax.experimental.pallas import tpu as pltpu
from jax.sharding import PartitionSpec as P

RELAX = 0.25
REACH = 3
HALO = 3 * REACH
PAD = 16
LANES = 128
FIRST = PAD - 8
THIRD, HALF = 1.0 / 3.0, 0.5

UPWIND = (-2.0, 15.0, -60.0, 20.0, 30.0, -3.0, 0.0)
CENTRAL = (-1.0, 9.0, -45.0, 0.0, 45.0, -9.0, 1.0)
DAMPING = (1.0, -6.0, 15.0, -20.0, 15.0, -6.0, 1.0)


def own_bands(cols):
    bands = np.zeros((2, LANES, LANES), np.float32)
    for col in range(cols):
        for offset in range(-REACH, REACH + 1):
            if 0 <= col + offset < cols:
                bands[0, col + offset, col] = UPWIND[offset + REACH]
                bands[1, col + offset, col] = -UPWIND[REACH - offset]
    return bands


def side_bands(count):
    bands = np.zeros((2, 2, 2 * LANES, 2 * LANES), np.float32)
    for side, (halo_at, edge_at) in enumerate(((0, -REACH), (-HALO, 0))):
        cells = [(halo_at + k, 0, k) for k in range(HALO)]
        cells += [(edge_at + k, LANES, k) for k in range(REACH)]
        for index in range(count):
            slot = index * HALO
            for source, source_half, source_lane in cells:
                for target, target_half, target_lane in cells:
                    offset = source - target
                    if abs(offset) > REACH or source_half == target_half == LANES:
                        continue
                    at = source_half + slot + source_lane, target_half + slot + target_lane
                    bands[side, 0][at] = UPWIND[offset + REACH]
                    bands[side, 1][at] = -UPWIND[REACH - offset]
    return bands


def iota(shape, dim):
    return lax.broadcasted_iota(jnp.int32, shape, dim)


def edge_weight(distance, width):
    dist = distance.astype(jnp.float32)
    inside = (dist >= 0.0) & (dist < width)
    return jnp.where(inside, jnp.square((width - dist) / width), 0.0)


def slots(count_f, count_l):
    return [(f, l, HALO * (f * count_l + l)) for f in range(count_f) for l in range(count_l)]


def pack_y_kernel(fields, first_round, second_round):
    count_f, count_l, rows, _ = fields.shape
    even = lax.rem(lax.axis_index("gy"), 2) == 0
    for f, l, slot in slots(count_f, count_l):
        top = fields[f, l, 0:HALO, :]
        bottom = fields[f, l, rows - HALO : rows, :]
        first_round[slot : slot + HALO, :] = jnp.where(even, bottom, top)
        second_round[slot : slot + HALO, :] = jnp.where(even, top, bottom)


def halo_rows(gy_count, first_round, second_round, slot):
    gy = lax.axis_index("gy")
    even = lax.rem(gy, 2) == 0
    first = first_round[slot : slot + HALO, :]
    second = second_round[slot : slot + HALO, :]
    north = jnp.where(gy == 0, 0.0, jnp.where(even, second, first))
    south = jnp.where(gy == gy_count - 1, 0.0, jnp.where(even, first, second))
    return north, south


def sent_starts(gx_count, cols):
    if gx_count == 2:
        return [jnp.where(lax.axis_index("gx") == 0, cols - HALO, 0)]
    return [cols - HALO, 0]


def side_ids(gx_count):
    if gx_count == 2:
        return [jnp.where(lax.axis_index("gx") == 0, 0, 1)]
    return [1, 0]


def edge_starts(gx_count, cols):
    return [jnp.where(side == 0, cols - REACH, 0) for side in side_ids(gx_count)]


def level_weights(coupling, wind_x, wind_y, l, count_f):
    speed, size = wind_y[l] / 60.0, jnp.abs(wind_y[l]) / 60.0
    taps = [size * DAMPING[k] - speed * CENTRAL[k] for k in range(2 * REACH + 1)]
    mix = [
        [coupling[f, l, g] + (taps[REACH] if f == g else 0.0) for g in range(count_f)]
        for f in range(count_f)
    ]
    return [tap for k, tap in enumerate(taps) if k != REACH], mix, -wind_x[l] / 60.0


def prepare_kernel(
    grid_sizes,
    fields,
    north,
    south,
    west,
    east,
    own_band,
    side_band,
    scale,
    widths,
    wind_x,
    wind_y,
    coupling,
    drive,
    relax,
    row_relax,
    inside,
    weights,
    lane_weights,
    own_matrix,
    *rest,
):
    gy_count, gx_count = grid_sizes
    sides = (len(rest) - 1) // 3
    payloads, side_drive, side_matrix = rest[:sides], rest[sides : 2 * sides], rest[2 * sides : -1]
    wide = rest[-1]
    count_f, count_l, rows, cols = fields.shape
    wide_rows = relax.shape[0]
    strip = north.shape[2]
    total_rows, total_cols = rows * gy_count, cols * gx_count
    gy, gx = lax.axis_index("gy"), lax.axis_index("gx")
    row_start, col_start = gy * rows, gx * cols
    width = [widths[s].astype(jnp.float32) for s in range(4)]
    lane = iota((8, LANES), 1)

    lane_rows = iota((rows, LANES), 1)
    starts = sent_starts(gx_count, cols)
    packed = [jnp.zeros((rows, LANES), jnp.float32) for _ in starts]
    if cols < LANES:
        wide[...] = jnp.zeros_like(wide)
    for f, l, slot in slots(count_f, count_l):
        if cols < LANES:
            wide[:, 0:cols] = fields[f, l]
            own = wide[...]
        else:
            own = fields[f, l]
        for n, start in enumerate(starts):
            moved = pltpu.roll(own, lax.rem(slot + LANES - start, LANES), 1)
            here = (lane_rows >= slot) & (lane_rows < slot + HALO)
            packed[n] = jnp.where(here, moved, packed[n])
    for payload, value in zip(payloads, packed):
        payload[...] = value

    def full(value):
        return jnp.full((8, LANES), value, jnp.float32)

    negative = jnp.zeros((1, 2 * LANES), jnp.bool_)
    double = lax.rem(iota((1, 2 * LANES), 1), LANES)
    lane_taps = [full(0.0) for _ in range(2 * REACH)]
    lane_mix = [full(0.0) for _ in range(2 * count_f - 1)]
    lane_speed = full(0.0)
    for l in range(count_l):
        taps, mix, speed = level_weights(coupling, wind_x, wind_y, l, count_f)
        flat = taps + [entry for line in mix for entry in line] + [speed]
        for n, entry in enumerate(flat):
            weights[l, n] = full(entry)
        own_matrix[l] = own_band[jnp.where(wind_x[l] < 0.0, 1, 0)]
        for f in range(count_f):
            slot = HALO * (f * count_l + l)
            here = (lane >= slot) & (lane < slot + HALO)
            lane_taps = [jnp.where(here, tap, old) for tap, old in zip(taps, lane_taps)]
            lane_speed = jnp.where(here, speed, lane_speed)
            for g in range(count_f):
                at = g - f + count_f - 1
                lane_mix[at] = jnp.where(here, mix[f][g], lane_mix[at])
            here = (double >= slot) & (double < slot + HALO)
            negative = negative | (here & (wind_x[l] < 0.0))
    for n, entry in enumerate(lane_taps + lane_mix + [lane_speed]):
        lane_weights[n] = entry
    for side, matrix in zip(side_ids(gx_count), side_matrix):
        matrix[...] = jnp.where(
            negative, side_band[side, 1].astype(jnp.float32), side_band[side, 0].astype(jnp.float32)
        ).astype(jnp.bfloat16)

    row_global = iota((wide_rows, LANES), 0) + (row_start - 8)
    row_weight = RELAX * (
        edge_weight(row_global, width[0]) + edge_weight(total_rows - 1 - row_global, width[1])
    )
    col_weight = RELAX * (
        edge_weight(lane + col_start, width[2])
        + edge_weight(total_cols - 1 - (lane + col_start), width[3])
    )
    row_relax[...] = row_weight
    relax[...] = row_weight + col_weight[0:1, :]
    inside[...] = jnp.where((row_global >= 0) & (row_global < total_rows), 1.0, 0.0)

    pos = iota((strip, LANES), 1)
    depth = iota((strip, LANES), 0)
    pick = jnp.concatenate([pos == depth, pos == depth + (cols - strip)], axis=0)
    pick = pick.astype(jnp.float32).astype(jnp.bfloat16)
    west_weight = RELAX * edge_weight(lane + col_start, width[2])
    east_weight = RELAX * edge_weight(total_cols - 1 - (lane + col_start), width[3])
    west_weight = jnp.where(lane < strip, west_weight, 0.0)
    east_weight = jnp.where((lane >= cols - strip) & (lane < cols), east_weight, 0.0)
    shift = lax.rem(8 + total_rows - row_start, total_rows)
    for f in range(count_f):
        for l in range(count_l):
            both = jnp.concatenate([west[f, l], east[f, l]], axis=0).astype(jnp.float32)
            both = pltpu.roll(both, shift, 1)[:, 0:LANES].astype(jnp.bfloat16)
            raw = lax.dot_general(
                both, pick, (((0,), (0,)), ((), ())), preferred_element_type=jnp.float32
            )
            factor = west_weight * scale[2, l, f] + east_weight * scale[3, l, f]
            drive[f, l] = raw[0:wide_rows] * factor[0:1, :]
    for ref in side_drive:
        ref[...] = jnp.zeros_like(ref)

    own_shift = lax.rem(total_cols - col_start, total_cols)
    for source, side, at, here in (
        (north, 0, 8, gy == 0),
        (south, 1, 8 + rows - strip, gy == gy_count - 1),
    ):

        @pl.when(here)
        def _(source=source, side=side, at=at):
            distance = depth if side == 0 else strip - 1 - depth
            weight = RELAX * edge_weight(distance, width[side])
            packed = [jnp.zeros((strip, LANES), jnp.float32) for _ in side_drive]
            for f, l, slot in slots(count_f, count_l):
                values = source[f, l].astype(jnp.float32)
                factor = weight * scale[side, l, f]
                own = pltpu.roll(values, own_shift, 1)[:, 0:LANES]
                drive[f, l, at : at + strip, :] = drive[f, l, at : at + strip, :] + factor * own
                for n, which in enumerate(side_ids(gx_count)):
                    begin = jnp.where(which == 0, cols, -HALO) + col_start
                    outer = pltpu.roll(
                        values, lax.rem(slot + 2 * total_cols - begin, total_cols), 1
                    )[:, 0:LANES]
                    packed[n] = jnp.where(
                        (pos >= slot) & (pos < slot + HALO), factor * outer, packed[n]
                    )
            for ref, value in zip(side_drive, packed):
                ref[at : at + strip, :] = value


def pack_x_kernel(grid_sizes, first_round, second_round, *rest):
    gy_count, gx_count = grid_sizes
    sides = (len(rest) - 1) // 2
    payloads, outs, ext = rest[:sides], rest[sides:-1], rest[-1]
    cols = first_round.shape[1]
    rows = payloads[0].shape[0]
    lane = iota((2 * PAD, LANES), 1)
    starts = sent_starts(gx_count, cols)
    packed = [jnp.zeros((2 * PAD, LANES), jnp.float32) for _ in starts]
    ext[...] = jnp.zeros_like(ext)
    for index in range(ext.shape[0]):
        slot = index * HALO
        north, south = halo_rows(gy_count, first_round, second_round, slot)
        ext[index, PAD - HALO : PAD, 0:cols] = north
        ext[index, PAD : PAD + HALO, 0:cols] = south
        for n, start in enumerate(starts):
            moved = pltpu.roll(ext[index], lax.rem(slot + LANES - start, LANES), 1)
            packed[n] = jnp.where((lane >= slot) & (lane < slot + HALO), moved, packed[n])
    for out, payload, value in zip(outs, payloads, packed):
        out[0:PAD, :] = value[0:PAD]
        out[PAD : PAD + rows, :] = payload[...]
        out[PAD + rows : 2 * PAD + rows, :] = value[PAD : 2 * PAD]


def loaded(weights, l, fac, count_f):
    flat = [fac * weights[l, n] for n in range(weights.shape[1])]
    taps, flat, speed = flat[: 2 * REACH], flat[2 * REACH : -1], flat[-1]
    return taps, [flat[f * count_f : (f + 1) * count_f] for f in range(count_f)], speed


def y_terms(rows_at, at, taps, total):
    offsets = [k for k in range(-REACH, REACH + 1) if k != 0]
    for tap, offset in zip(taps, offsets):
        total = total + tap * rows_at(at + offset)
    return total


def cell_terms(src, l, f, at, centers, weight, taps, mix, total):
    for g, center in enumerate(centers):
        total = total + (mix[f][g] - weight if g == f else mix[f][g]) * center
    return y_terms(lambda row: src[f, l, pl.ds(row, 8), :], at, taps, total)


def split(value):
    high = value.astype(jnp.bfloat16)
    return high, (value - high.astype(jnp.float32)).astype(jnp.bfloat16)


def x_divergence(src, l, first, height, matrix, xdiv):
    count_f = src.shape[0]
    whole = src[:, l, first : first + height, :].reshape(count_f * height, LANES)
    both = jnp.concatenate(split(whole), axis=1)
    twice = jnp.concatenate([matrix[l], matrix[l]], axis=0)
    moved = jnp.dot(both, twice, preferred_element_type=jnp.float32)
    xdiv[:, 0:height, :] = moved.reshape(count_f, height, LANES)


def begin_kernel(
    grid_sizes,
    fields,
    first_round,
    second_round,
    drive,
    relax,
    weights,
    own_matrix,
    part_one,
    base_two,
    base_three,
    *rest,
):
    gy_count, gx_count = grid_sizes
    edges, state, xdiv = rest[:-2], rest[-2], rest[-1]
    count_f, count_l, rows, cols = fields.shape
    wide_rows = relax.shape[0]
    pad_rows = jnp.zeros((PAD, LANES), jnp.float32)
    for f, l, slot in slots(count_f, count_l):
        north, south = halo_rows(gy_count, first_round, second_round, slot)
        if cols < LANES:
            state[f, l] = jnp.zeros(state.shape[2:], jnp.float32)
        else:
            state[f, l, 0:PAD, :] = pad_rows
            state[f, l, PAD + rows : 2 * PAD + rows, :] = pad_rows
        state[f, l, PAD - HALO : PAD, 0:cols] = north
        state[f, l, PAD : PAD + rows, 0:cols] = fields[f, l]
        state[f, l, PAD + rows : PAD + rows + HALO, 0:cols] = south
    lane = iota((wide_rows, LANES), 1)
    for edge, start in zip(edges, edge_starts(gx_count, cols)):
        packed = jnp.zeros((wide_rows, LANES), jnp.float32)
        near = (lane >= start) & (lane < start + REACH)
        for f, l, slot in slots(count_f, count_l):
            kept = jnp.where(near, state[f, l, FIRST : FIRST + wide_rows, :], 0.0)
            packed = packed + pltpu.roll(kept, lax.rem(slot + LANES - start, LANES), 1)
        edge[...] = packed
    for l in range(count_l):
        x_divergence(state, l, FIRST, wide_rows, own_matrix, xdiv)
        taps, mix, speed = loaded(weights, l, THIRD, count_f)

        def group(n, _):
            at = pl.multiple_of(FIRST + n * 8, 8)
            to = pl.multiple_of(n * 8, 8)
            centers = [state[g, l, pl.ds(at, 8), :] for g in range(count_f)]
            weight = THIRD * relax[pl.ds(to, 8), :]
            for f in range(count_f):
                forced = drive[f, l, pl.ds(to, 8), :]
                base_two[f, l, pl.ds(to, 8), :] = centers[f] + HALF * forced
                base_three[f, l, pl.ds(to, 8), :] = centers[f] + forced
                total = centers[f] + THIRD * forced + speed * xdiv[f, pl.ds(to, 8), :]
                total = cell_terms(state, l, f, at, centers, weight, taps, mix, total)
                part_one[f, l, pl.ds(to, 8), :] = total
            return 0

        lax.fori_loop(0, wide_rows // 8, group, 0)


def finish_kernel(grid_sizes, sides, *refs):
    gy_count, gx_count = grid_sizes
    halos, edges, side_drive, side_matrix = (
        refs[n * sides : (n + 1) * sides] for n in range(4)
    )
    (
        part_one,
        base_two,
        base_three,
        relax,
        row_relax,
        inside,
        weights,
        lane_weights,
        own_matrix,
        out,
        own_one,
        own_two,
        halo_one,
        halo_two,
        edge_next,
        halo_div,
        edge_add,
        xdiv,
    ) = refs[4 * sides :]
    count_f, count_l, rows, cols = out.shape
    wide_rows = relax.shape[0]
    groups = wide_rows // 8
    gy, gx = lax.axis_index("gy"), lax.axis_index("gx")
    starts = edge_starts(gx_count, cols)
    exists = [None] if sides == 1 else [gx > 0, gx < gx_count - 1]
    lane = iota((8, LANES), 1)
    near = [(lane >= start) & (lane < start + REACH) for start in starts]
    zeros = jnp.zeros((8, LANES), jnp.float32)

    def halo_products(halo, edge, matrix, s, fac, first, height):
        speed = lane_weights[lane_weights.shape[0] - 1][0:1, :]
        rows_in = halo[pl.ds(first, height), :]
        if edge is None:
            both = jnp.concatenate(split(rows_in), axis=0)
            moved = jnp.dot(
                both, matrix[0:LANES, LANES:], preferred_element_type=jnp.float32
            )
            add = moved[0:height] + moved[height:]
        else:
            rows_in = jnp.concatenate([rows_in, edge], axis=1)
            both = jnp.concatenate(split(rows_in), axis=0)
            moved = jnp.dot(both, matrix[...], preferred_element_type=jnp.float32)
            moved = moved[0:height] + moved[height:]
            halo_div[s] = speed * moved[:, 0:LANES]
            add = moved[:, LANES:]
        edge_add[s, 0:height, :] = (fac * speed) * add

    def halo_section(halo, halo_next, s, fac):
        count = 2 * count_f - 1
        for n in range(groups):
            at, to = FIRST + n * 8, n * 8
            center = halo[at : at + 8, :]
            rate = side_drive[s][to : to + 8, :] + halo_div[s, to : to + 8, :]
            rate = rate - row_relax[to : to + 8, :] * center
            for d in range(count):
                moved = center
                if d != count_f - 1:
                    step = (d - (count_f - 1)) * HALO * count_l
                    moved = pltpu.roll(center, -step % LANES, 1)
                rate = rate + lane_weights[2 * REACH + d] * moved
            taps = [lane_weights[k] for k in range(2 * REACH)]
            rate = y_terms(lambda row: halo[row : row + 8, :], at, taps, rate)
            value = halos[s][at : at + 8, :] + fac * rate
            kept = inside[to : to + 8, :]
            if exists[s] is not None:
                kept = jnp.where(exists[s], kept, 0.0)
            halo_next[s, at : at + 8, :] = value * kept

    def from_halo(total, slot, to):
        for s, start in enumerate(starts):
            shift = lax.rem(start + LANES - slot, LANES)
            moved = pltpu.roll(edge_add[s, pl.ds(to, 8), :], shift, 1)
            total = total + jnp.where(near[s], moved, 0.0)
        return total

    def keep_edges(packed, value, slot):
        for s, start in enumerate(starts):
            moved = pltpu.roll(
                jnp.where(near[s], value, 0.0), lax.rem(slot + LANES - start, LANES), 1
            )
            packed[s] = packed[s] + moved

    def outside_rows(own, section):
        for row, here in ((0, gy == 0), (rows + 8, gy == gy_count - 1)):

            @pl.when(here)
            def _(row=row):
                own[:, :, FIRST + row : FIRST + row + 8, :] = jnp.zeros(
                    (count_f, count_l, 8, LANES), jnp.float32
                )
                for s in range(sides):
                    for l in range(count_l):
                        edge_next[section, s, l, row : row + 8, :] = zeros

    for s in range(sides):
        halo_products(halos[s], edges[s][...], side_matrix[s], s, THIRD, FIRST, wide_rows)
        halo_section(halos[s], halo_one, s, THIRD)
    for l in range(count_l):

        def group(n, _):
            at = pl.multiple_of(FIRST + n * 8, 8)
            to = pl.multiple_of(n * 8, 8)
            packed = [zeros] * sides
            for f in range(count_f):
                slot = HALO * (f * count_l + l)
                value = from_halo(part_one[f, l, pl.ds(to, 8), :], slot, to)
                own_one[f, l, pl.ds(at, 8), :] = value
                keep_edges(packed, value, slot)
            for s in range(sides):
                edge_next[0, s, l, pl.ds(to, 8), :] = packed[s]
            return 0

        lax.fori_loop(0, groups, group, 0)
    outside_rows(own_one, 0)

    def edges_of(section, s):
        return sum(edge_next[section, s, l] for l in range(count_l))

    for s in range(sides):
        halo_products(
            halo_one.at[s], edges_of(0, s), side_matrix[s], s, HALF, FIRST, wide_rows
        )
        halo_section(halo_one.at[s], halo_two, s, HALF)
    for l in range(count_l):
        x_divergence(own_one, l, FIRST, wide_rows, own_matrix, xdiv)
        taps, mix, speed = loaded(weights, l, HALF, count_f)

        def group(n, _):
            at = pl.multiple_of(FIRST + n * 8, 8)
            to = pl.multiple_of(n * 8, 8)
            centers = [own_one[g, l, pl.ds(at, 8), :] for g in range(count_f)]
            weight = HALF * relax[pl.ds(to, 8), :]
            for f in range(count_f):
                total = base_two[f, l, pl.ds(to, 8), :] + speed * xdiv[f, pl.ds(to, 8), :]
                total = from_halo(total, HALO * (f * count_l + l), to)
                own_two[f, l, pl.ds(at, 8), :] = cell_terms(
                    own_one, l, f, at, centers, weight, taps, mix, total
                )
            return 0

        lax.fori_loop(0, groups, group, 0)
    for row, here in ((0, gy == 0), (rows + 8, gy == gy_count - 1)):

        @pl.when(here)
        def _(row=row):
            own_two[:, :, FIRST + row : FIRST + row + 8, :] = jnp.zeros(
                (count_f, count_l, 8, LANES), jnp.float32
            )

    for s in range(sides):
        halo_products(halo_two.at[s], None, side_matrix[s], s, 1.0, PAD, rows)
    for l in range(count_l):
        x_divergence(own_two, l, PAD, rows, own_matrix, xdiv)
        taps, mix, speed = loaded(weights, l, 1.0, count_f)

        def group(n, _):
            at = pl.multiple_of(PAD + n * 8, 8)
            to = pl.multiple_of(n * 8, 8)
            centers = [own_two[g, l, pl.ds(at, 8), :] for g in range(count_f)]
            weight = relax[pl.ds(to + 8, 8), :]
            for f in range(count_f):
                total = base_three[f, l, pl.ds(to + 8, 8), :] + speed * xdiv[f, pl.ds(to, 8), :]
                total = from_halo(total, HALO * (f * count_l + l), to)
                total = cell_terms(own_two, l, f, at, centers, weight, taps, mix, total)
                out[f, l, pl.ds(to, 8), :] = total[:, 0:cols]
            return 0

        lax.fori_loop(0, rows // 8, group, 0)


def pair_rounds(gy_count, gx_count):
    rounds = []
    for start in (0, 1):
        partner = {}
        for low in range(start, gy_count - 1, 2):
            partner[low], partner[low + 1] = low + 1, low
        pairs = []
        for y in range(gy_count):
            for x in range(gx_count):
                if y in partner:
                    pairs.append((y * gx_count + x, partner[y] * gx_count + x))
                elif gx_count % 2 == 0:
                    pairs.append((y * gx_count + x, y * gx_count + (x ^ 1)))
        rounds.append(pairs)
    return rounds


def local(
    gy_count, gx_count, fields, wind_x, wind_y, coupling, north, south, west, east, strip_scale, widths
):
    count_f, count_l, rows, cols = fields.shape
    ext_rows = rows + 2 * PAD
    grid_sizes = (gy_count, gx_count)
    packed_rows = -(-HALO * count_f * count_l // 8) * 8
    vmem = pl.BlockSpec(memory_space=pltpu.VMEM)
    smem = pl.BlockSpec(memory_space=pltpu.SMEM)
    f32 = functools.partial(jax.ShapeDtypeStruct, dtype=jnp.float32)

    def call(body, name, out_shape, inputs, scratch=(), limit=4):
        several = isinstance(out_shape, tuple)
        return pl.pallas_call(
            body,
            out_shape=out_shape,
            in_specs=[space for _, space in inputs],
            out_specs=(vmem,) * len(out_shape) if several else vmem,
            scratch_shapes=list(scratch),
            compiler_params=pltpu.CompilerParams(vmem_limit_bytes=limit << 20),
            name=name,
        )(*[value for value, _ in inputs])

    def inputs(space, *values):
        return [(value, space) for value in values]

    strip_shape = f32((packed_rows, cols))
    sent_first, sent_second = call(
        pack_y_kernel, "pack_y", (strip_shape, strip_shape), inputs(vmem, fields)
    )
    first_pairs, second_pairs = pair_rounds(gy_count, gx_count)
    first_round = lax.ppermute(sent_first, ("gy", "gx"), first_pairs)
    second_round = lax.ppermute(sent_second, ("gy", "gx"), second_pairs)

    mixing = jnp.transpose(coupling, (1, 0, 2))
    scales = jnp.transpose(strip_scale, (0, 2, 1))
    sides = 1 if gx_count == 2 else 2
    wide_rows = rows + 16
    state_shape = (count_f, count_l, ext_rows, LANES)
    wide_shape = (count_f, count_l, wide_rows, LANES)
    plane = f32((wide_rows, LANES))
    matrix = functools.partial(jax.ShapeDtypeStruct, dtype=jnp.bfloat16)
    entries = 2 * REACH + count_f * count_f + 1
    lane_entries = 2 * REACH + 2 * count_f
    prepared = call(
        functools.partial(prepare_kernel, grid_sizes),
        "prepare",
        (f32(wide_shape), plane, plane, plane)
        + (f32((count_l, entries, 8, LANES)), f32((lane_entries, 8, LANES)))
        + (matrix((count_l, LANES, LANES)),)
        + (f32((rows, LANES)),) * sides
        + (plane,) * sides
        + (matrix((2 * LANES, 2 * LANES)),) * sides,
        inputs(vmem, fields, north, south, jnp.swapaxes(west, 2, 3), jnp.swapaxes(east, 2, 3))
        + inputs(
            vmem,
            jnp.asarray(own_bands(cols), jnp.bfloat16),
            jnp.asarray(side_bands(count_f * count_l), jnp.bfloat16),
        )
        + inputs(smem, scales, widths, wind_x, wind_y, mixing),
        scratch=[pltpu.VMEM((rows, LANES), jnp.float32)],
    )
    drive, relax, row_relax, inside, weights, lane_weights, own_matrix = prepared[:7]
    payloads, side_drive, side_matrix = (
        prepared[7 + n * sides : 7 + (n + 1) * sides] for n in range(3)
    )

    sent = call(
        functools.partial(pack_x_kernel, grid_sizes),
        "pack_x",
        (f32((ext_rows, LANES)),) * sides,
        inputs(vmem, first_round, second_round, *payloads),
        scratch=[pltpu.VMEM((count_f * count_l, 2 * PAD, LANES), jnp.float32)],
    )
    forward = [(i, i + 1) for i in range(gx_count - 1)]
    backward = [(b, a) for a, b in forward]
    if sides == 1:
        halos = [lax.ppermute(sent[0], "gx", forward + backward)]
    else:
        halos = [lax.ppermute(sent[0], "gx", forward), lax.ppermute(sent[1], "gx", backward)]

    begun = call(
        functools.partial(begin_kernel, grid_sizes),
        "begin",
        (f32(wide_shape),) * 3 + (plane,) * sides,
        inputs(vmem, fields, first_round, second_round, drive, relax, weights, own_matrix),
        scratch=[
            pltpu.VMEM(state_shape, jnp.float32),
            pltpu.VMEM((count_f, wide_rows, LANES), jnp.float32),
        ],
    )
    halo_state = pltpu.VMEM((sides, ext_rows, LANES), jnp.float32)
    halo_plane = pltpu.VMEM((sides, wide_rows, LANES), jnp.float32)
    return call(
        functools.partial(finish_kernel, grid_sizes, sides),
        "finish",
        f32(fields.shape),
        inputs(vmem, *halos, *begun[3:], *side_drive, *side_matrix, *begun[:3])
        + inputs(vmem, relax, row_relax, inside, weights, lane_weights, own_matrix),
        scratch=[
            pltpu.VMEM(state_shape, jnp.float32),
            pltpu.VMEM(state_shape, jnp.float32),
            halo_state,
            halo_state,
            pltpu.VMEM((1, sides, count_l, wide_rows, LANES), jnp.float32),
            halo_plane,
            halo_plane,
            pltpu.VMEM((count_f, wide_rows, LANES), jnp.float32),
        ],
        limit=8,
    )


def solution(mesh):
    return jax.shard_map(
        functools.partial(local, mesh.shape["gy"], mesh.shape["gx"]),
        mesh=mesh,
        in_specs=(
            P("mem", None, "gy", "gx"),
            P("mem"),
            P("mem"),
            P(),
            P("mem", None, None, None),
            P("mem", None, None, None),
            P("mem", None, None, None),
            P("mem", None, None, None),
            P("mem", None, None),
            P(),
        ),
        out_specs=P("mem", None, "gy", "gx"),
        check_vma=False,
    )
```

time: 19.3 us -> 20.9 us (1.083)
  Pallas kernels: 8.67 us -> 10.8 us
  local copies, waits for them, and re-layouts: 2.93 us -> 2.05 us
  waiting for transfers between devices: 1.26 us -> 1.53 us
    pallas_call x5, Pallas kernels: 8.67 us -> 10.8 us  [call(): pl.pallas_call(body, out_shape=out_shape, in_specs=[space for _, space in...]
    unnamed x24 -> x26, local copies, waits for them, and re-layouts: 2.93 us -> 2.05 us
    ppermute x1, waiting for transfers between devices: 0.48 us -> 1.33 us  [local(): halos = [lax.ppermute(sent[0], 'gx', forward + backward)]]
    ppermute x1, waiting for transfers between devices: 0.77 us -> 0.2 us  [local(): second_round = lax.ppermute(sent_second, ('gy', 'gx'), second_pairs)]
  transfers between devices with their start and end apart: 3 -> 3, of which waited for: 2 -> 2; matrix products, arithmetic and copies ran while one was open for 0% -> 0% of each run, Pallas kernels for 14% -> 12%
where the time goes in v4:
time: 20.9 us; the launch traced here: 20.7 us
  Pallas kernels  10.8 us (52%)
  starting transfers between devices  6.16 us (29%)
  local copies, waits for them, and re-layouts  2.05 us (10%)
  waiting for transfers between devices  1.53 us (7%)
    pallas_call x5, Pallas kernels, call(): pl.pallas_call(body, out_shape=out_shape, in_specs=[space for _, space in...  10.8 us
    ppermute x1, starting transfers between devices, local(): first_round = lax.ppermute(sent_first, ('gy', 'gx'), first_pairs)  3.12 us
    unnamed x26, local copies, waits for them, and re-layouts  2.05 us
    ppermute x1, starting transfers between devices, local(): halos = [lax.ppermute(sent[0], 'gx', forward + backward)]  1.56 us
    ppermute x1, starting transfers between devices, local(): second_round = lax.ppermute(sent_second, ('gy', 'gx'), second_pairs)  1.49 us
    ppermute x1, waiting for transfers between devices, local(): halos = [lax.ppermute(sent[0], 'gx', forward + backward)]  1.33 us
  transfers between devices with their start and end apart: 3, of which 2 were waited for; matrix products, arithmetic and copies ran while one was open for 0% of the time, Pallas kernels for 12%

profile of v4, /device:TPU:0, one launch (start us, length us, event | category | flops | bytes accessed | tf_op | source)
XLA Modules:
  0.0 20.7 jit_solution(9252521061353202123)
XLA Ops:
  0.0 0.0 copy-start
  0.0 1.0 %copy-done = f32[5,2,64,128]{3,2,1,0:T(8,128)S(1)} copy-done((f32[5,2,64,128]{3,2,1,0:T(8,128)S(1)}, f32[5,2,64,128]{3,2,1,0:T(8,128)}, u32[]{:S(2)}) %copy-start) | copy-done | bytes 327704
  1.0 0.0 copy-start.3
  1.0 0.0 copy-start.4
  1.0 0.0 copy-start.7
  1.0 0.0 copy-start.10
  1.0 0.0 copy-start.11
  1.0 0.0 copy-start.12
  1.1 0.0 copy-start.8
  1.1 3.1 %collective-permute-start = (f32[96,128]{1,0:T(8,128)S(1)}, f32[96,128]{1,0:T(8,128)S(1)}, u32[]{:S(2)}, u32[]{:S(2)}) collective-permute-start(f32[96,128]{1,0:T(8,128)S(1)} %get-tuple-element.21), channel_id=1, source_target_pairs={{0,2},{1,3},{2,0},{3,1},{4,6},{5,7},{6,4},{7,5},{8,10},{9,11},{10,... | collective-permute-start | bytes 147464 | tf_op jit(solution)/shard_map/ppermute | solution.py:597
  4.2 1.5 %collective-permute-start.1 = (f32[96,128]{1,0:T(8,128)S(1)}, f32[96,128]{1,0:T(8,128)S(1)}, u32[]{:S(2)}, u32[]{:S(2)}) collective-permute-start(f32[96,128]{1,0:T(8,128)S(1)} %get-tuple-element.22), channel_id=1, source_target_pairs={{0,1},{1,0},{2,4},{3,5},{4,2},{5,3},{6,7},{7,6},{8,9},{9,8},{10,12... | collective-permute-start | bytes 147464 | tf_op jit(solution)/shard_map/ppermute | solution.py:598
  5.7 0.0 copy-done.3
  5.7 0.0 copy-done.4
  5.7 0.0 copy-done.5
  5.7 0.0 copy-done.6
  5.7 0.0 copy-done.7
  5.7 0.0 copy-done.10
  5.7 0.0 copy-done.11
  5.7 0.0 copy-done.12
  5.7 0.0 copy-done.8
  5.7 0.0 copy-done.9
  5.8 0.0 copy-start.2
  5.8 1.0 %copy-done.2 = bf16[2,2,256,256]{3,2,1,0:T(8,128)(2,1)S(1)} copy-done((bf16[2,2,256,256]{3,2,1,0:T(8,128)(2,1)S(1)}, bf16[2,2,256,256]{3,2,1,0:T(8,128)(2,1)}, u32[]{:S(2)}) %copy-start.2) | copy-done | bytes 524312
  6.8 1.3 %prepare.1 = (f32[5,2,80,128]{3,2,1,0:T(8,128)S(1)}, f32[80,128]{1,0:T(8,128)S(1)}, f32[80,128]{1,0:T(8,128)S(1)}, f32[80,128]{1,0:T(8,128)S(1)}, f32[2,32,8,128...) custom-call(f32[5,2,64,128]{3,2,1,0:T(8,128)S(1)} %copy-done, ...), custom_call_target="tpu_custom_call" | custom-call | tf_op jit(solution)/shard_map/prepare/pallas_call | solution.py:579
  8.1 0.0 collective-permute-done.first_round
  8.1 0.2 collective-permute-done.1.second_round
  8.3 0.1 pack_x.1
  8.4 1.6 %collective-permute-start.2 = (f32[96,128]{1,0:T(8,128)S(1)}, f32[96,128]{1,0:T(8,128)S(1)}, u32[]{:S(2)}, u32[]{:S(2)}) collective-permute-start(f32[96,128]{1,0:T(8,128)S(1)} %pack_x.1), channel_id=1, source_target_pairs={{0,1},{1,0},{2,3},{3,2},{4,5},{5,4},{6,7},{7,6},{8,9},{9,8},{10,11... | collective-permute-start | bytes 147464 | tf_op jit(solution)/shard_map/ppermute | solution.py:643
  10.0 0.0 copy-done.1
  10.0 1.3 %begin.1 = (f32[5,2,80,128]{3,2,1,0:T(8,128)S(1)}, f32[5,2,80,128]{3,2,1,0:T(8,128)S(1)}, f32[5,2,80,128]{3,2,1,0:T(8,128)S(1)}, f32[80,128]{1,0:T(8,128)S(1)}) custom-call(f32[5,2,64,128]{3,2,1,0:T(8,128)S(1)} %copy-done.1, f32[96,128]{1,0:T(8,128)S(1)} %collective-permute-done.first_round, f32[96,128]{1,0:T(8,128)S(1)} %collective-permute-done.1.second_round, ...), custom_call_target="tpu_custom_call" | custom-call | tf_op jit(solution)/shard_map/begin/pallas_call | solution.py:579
  11.2 1.3 %collective-permute-done.2.refs_0_ = f32[96,128]{1,0:T(8,128)S(1)} collective-permute-done((f32[96,128]{1,0:T(8,128)S(1)}, f32[96,128]{1,0:T(8,128)S(1)}, u32[]{:S(2)}, u32[]{:S(2)}) %collective-permute-start.2) | collective-permute-done | bytes 49184 | tf_op jit(solution)/shard_map/ppermute | solution.py:643
  12.6 8.1 %finish.1 = f32[5,2,64,128]{3,2,1,0:T(8,128)} custom-call(f32[96,128]{1,0:T(8,128)S(1)} %collective-permute-done.2.refs_0_, f32[80,128]{1,0:T(8,128)S(1)} %get-tuple-element.28.refs_1_, f32[80,128]{1,0:T(8,128)S(1)} %get-tuple-element.29.refs_2_, bf16[256,256]{1,0:T(8,128)(2,1)S(1)} %get-tuple-element.30.refs_3_, ...), custom_call_target="tpu_custom_call" | custom-call | tf_op jit(solution)/shard_map/finish/pallas_call | solution.py:579
  (5 shorter events, 0.0 us)
Async XLA Ops:
  0.0 1.0 %copy-start = (f32[5,2,64,128]{3,2,1,0:T(8,128)S(1)}, f32[5,2,64,128]{3,2,1,0:T(8,128)}, u32[]{:S(2)}) copy-start(f32[5,2,64,128]{3,2,1,0:T(8,128)} %fields.5) | copy-start | bytes 983044
  1.0 4.7 %copy-start.3 = (bf16[2,128,128]{2,1,0:T(8,128)(2,1)S(1)}, bf16[2,128,128]{2,1,0:T(8,128)(2,1)}, u32[]{:S(2)}) copy-start(bf16[2,128,128]{2,1,0:T(8,128)(2,1)} %constant.4.clone.own_band) | copy-start | bytes 196612
  1.0 4.7 %copy-start.4 = (bf16[5,2,8,256]{3,2,1,0:T(8,128)(2,1)S(1)}, bf16[5,2,8,256]{3,2,1,0:T(8,128)(2,1)}, u32[]{:S(2)}) copy-start(bf16[5,2,8,256]{3,2,1,0:T(8,128)(2,1)} %north.1) | copy-start | bytes 122884
  1.0 4.7 %copy-start.5 = (bf16[5,2,8,256]{3,2,1,0:T(8,128)(2,1)S(1)}, bf16[5,2,8,256]{3,2,1,0:T(8,128)(2,1)}, u32[]{:S(2)}) copy-start(bf16[5,2,8,256]{3,2,1,0:T(8,128)(2,1)} %south.1) | copy-start | bytes 122884
  1.0 4.7 %copy-start.6 = (bf16[5,2,256,8]{2,3,1,0:T(8,128)(2,1)S(1)}, bf16[5,2,256,8]{2,3,1,0:T(8,128)(2,1)}, u32[]{:S(2)}) copy-start(bf16[5,2,256,8]{2,3,1,0:T(8,128)(2,1)} %param.18) | copy-start | bytes 122884
  1.0 4.7 %copy-start.7 = (bf16[5,2,256,8]{2,3,1,0:T(8,128)(2,1)S(1)}, bf16[5,2,256,8]{2,3,1,0:T(8,128)(2,1)}, u32[]{:S(2)}) copy-start(bf16[5,2,256,8]{2,3,1,0:T(8,128)(2,1)} %param.19) | copy-start | bytes 122884
  1.0 4.7 %copy-start.10 = (s32[4]{0:T(128)S(1)}, s32[4]{0:T(128)}, u32[]{:S(2)}) copy-start(s32[4]{0:T(128)} %widths.1) | copy-start | bytes 52
  1.0 4.7 %copy-start.11 = (f32[2]{0:T(128)S(1)}, f32[2]{0:T(128)}, u32[]{:S(2)}) copy-start(f32[2]{0:T(128)} %wind_x.1) | copy-start | bytes 28
  1.0 4.7 %copy-start.12 = (f32[2]{0:T(128)S(1)}, f32[2]{0:T(128)}, u32[]{:S(2)}) copy-start(f32[2]{0:T(128)} %wind_y.1) | copy-start | bytes 28
  1.1 4.7 %copy-start.8 = (f32[2,5,5]{2,0,1:T(2,128)S(1)}, f32[2,5,5]{2,0,1:T(2,128)}, u32[]{:S(2)}) copy-start(f32[2,5,5]{2,0,1:T(2,128)} %param.15) | copy-start | bytes 604
  1.1 7.0 %collective-permute-start = (f32[96,128]{1,0:T(8,128)S(1)}, f32[96,128]{1,0:T(8,128)S(1)}, u32[]{:S(2)}, u32[]{:S(2)}) collective-permute-start(f32[96,128]{1,0:T(8,128)S(1)} %get-tuple-element.21), channel_id=1, source_target_pairs={{0,2},{1,3},{2,0},{3,1},{4,6},{5,7},{6,4},{7,5},{8,10},{9,11},{10,... | collective-permute-start | bytes 147464 | tf_op jit(solution)/shard_map/ppermute | solution.py:597
  4.2 1.6 %copy-start.9 = (f32[4,5,2]{1,2,0:T(2,128)S(1)}, f32[4,5,2]{1,2,0:T(2,128)}, u32[]{:S(2)}) copy-start(f32[4,5,2]{1,2,0:T(2,128)} %param.20) | copy-start | bytes 484
  4.2 4.1 %collective-permute-start.1 = (f32[96,128]{1,0:T(8,128)S(1)}, f32[96,128]{1,0:T(8,128)S(1)}, u32[]{:S(2)}, u32[]{:S(2)}) collective-permute-start(f32[96,128]{1,0:T(8,128)S(1)} %get-tuple-element.22), channel_id=1, source_target_pairs={{0,1},{1,0},{2,4},{3,5},{4,2},{5,3},{6,7},{7,6},{8,9},{9,8},{10,12... | collective-permute-start | bytes 147464 | tf_op jit(solution)/shard_map/ppermute | solution.py:598
  5.8 1.0 %copy-start.2 = (bf16[2,2,256,256]{3,2,1,0:T(8,128)(2,1)S(1)}, bf16[2,2,256,256]{3,2,1,0:T(8,128)(2,1)}, u32[]{:S(2)}) copy-start(bf16[2,2,256,256]{3,2,1,0:T(8,128)(2,1)} %constant.5.clone.side_band) | copy-start | bytes 1572868
  6.8 3.2 %copy-start.1 = (f32[5,2,64,128]{3,2,1,0:T(8,128)S(1)}, f32[5,2,64,128]{3,2,1,0:T(8,128)}, u32[]{:S(2)}) copy-start(f32[5,2,64,128]{3,2,1,0:T(8,128)} %fields.5) | copy-start | bytes 983044
  8.4 4.2 %collective-permute-start.2 = (f32[96,128]{1,0:T(8,128)S(1)}, f32[96,128]{1,0:T(8,128)S(1)}, u32[]{:S(2)}, u32[]{:S(2)}) collective-permute-start(f32[96,128]{1,0:T(8,128)S(1)} %pack_x.1), channel_id=1, source_target_pairs={{0,1},{1,0},{2,3},{3,2},{4,5},{5,4},{6,7},{7,6},{8,9},{9,8},{10,11... | collective-permute-start | bytes 147464 | tf_op jit(solution)/shard_map/ppermute | solution.py:643

commit v5 on v4

--- a/solution.py
+++ b/solution.py
@@ -367,7 +367,7 @@
                 part_one[f, l, pl.ds(to, 8), :] = total
             return 0
 
-        lax.fori_loop(0, wide_rows // 8, group, 0)
+        lax.fori_loop(0, wide_rows // 8, group, 0, unroll=True)
 
 
 def finish_kernel(grid_sizes, sides, *refs):
@@ -488,7 +488,7 @@
                 edge_next[0, s, l, pl.ds(to, 8), :] = packed[s]
             return 0
 
-        lax.fori_loop(0, groups, group, 0)
+        lax.fori_loop(0, groups, group, 0, unroll=True)
     outside_rows(own_one, 0)
 
     def edges_of(section, s):
@@ -516,7 +516,7 @@
                 )
             return 0
 
-        lax.fori_loop(0, groups, group, 0)
+        lax.fori_loop(0, groups, group, 0, unroll=True)
     for row, here in ((0, gy == 0), (rows + 8, gy == gy_count - 1)):
 
         @pl.when(here)
@@ -543,7 +543,7 @@
                 out[f, l, pl.ds(to, 8), :] = total[:, 0:cols]
             return 0
 
-        lax.fori_loop(0, rows // 8, group, 0)
+        lax.fori_loop(0, rows // 8, group, 0, unroll=True)
 
 
 def pair_rounds(gy_count, gx_count):

time: 20.9 us -> 15.7 us (0.75)
  Pallas kernels: 10.8 us -> 5.12 us
  waiting for transfers between devices: 1.53 us -> 2.01 us
    pallas_call x5, Pallas kernels: 10.8 us -> 5.12 us  [call(): pl.pallas_call(body, out_shape=out_shape, in_specs=[space for _, space in...]
    ppermute x1, waiting for transfers between devices: 1.33 us -> 1.81 us  [local(): halos = [lax.ppermute(sent[0], 'gx', forward + backward)]]
  transfers between devices with their start and end apart: 3 -> 3, of which waited for: 2 -> 2; matrix products, arithmetic and copies ran while one was open for 0% -> 0% of each run, Pallas kernels for 12% -> 13%
where the time goes in v5:
time: 15.7 us; the launch traced here: 15.5 us
  starting transfers between devices  6.16 us (39%)
  Pallas kernels  5.12 us (33%)
  local copies, waits for them, and re-layouts  2.05 us (13%)
  waiting for transfers between devices  2.01 us (13%)
    pallas_call x5, Pallas kernels, call(): pl.pallas_call(body, out_shape=out_shape, in_specs=[space for _, space in...  5.12 us
    ppermute x1, starting transfers between devices, local(): first_round = lax.ppermute(sent_first, ('gy', 'gx'), first_pairs)  3.12 us
    unnamed x26, local copies, waits for them, and re-layouts  2.05 us
    ppermute x1, waiting for transfers between devices, local(): halos = [lax.ppermute(sent[0], 'gx', forward + backward)]  1.81 us
    ppermute x1, starting transfers between devices, local(): halos = [lax.ppermute(sent[0], 'gx', forward + backward)]  1.56 us
    ppermute x1, starting transfers between devices, local(): second_round = lax.ppermute(sent_second, ('gy', 'gx'), second_pairs)  1.49 us
  transfers between devices with their start and end apart: 3, of which 2 were waited for; matrix products, arithmetic and copies ran while one was open for 0% of the time, Pallas kernels for 13%

profile of v5, /device:TPU:0, one launch (start us, length us, event | category | flops | bytes accessed | tf_op | source)
XLA Modules:
  0.0 15.5 jit_solution(9476633075826587401)
XLA Ops:
  0.0 0.0 copy-start
  0.0 1.0 %copy-done = f32[5,2,64,128]{3,2,1,0:T(8,128)S(1)} copy-done((f32[5,2,64,128]{3,2,1,0:T(8,128)S(1)}, f32[5,2,64,128]{3,2,1,0:T(8,128)}, u32[]{:S(2)}) %copy-start) | copy-done | bytes 327704
  1.0 0.0 copy-start.3
  1.0 0.0 copy-start.4
  1.0 0.0 copy-start.7
  1.0 0.0 copy-start.10
  1.0 0.0 copy-start.11
  1.0 0.0 copy-start.12
  1.1 0.0 copy-start.8
  1.1 3.1 %collective-permute-start = (f32[96,128]{1,0:T(8,128)S(1)}, f32[96,128]{1,0:T(8,128)S(1)}, u32[]{:S(2)}, u32[]{:S(2)}) collective-permute-start(f32[96,128]{1,0:T(8,128)S(1)} %get-tuple-element.21), channel_id=1, source_target_pairs={{0,2},{1,3},{2,0},{3,1},{4,6},{5,7},{6,4},{7,5},{8,10},{9,11},{10,... | collective-permute-start | bytes 147464 | tf_op jit(solution)/shard_map/ppermute | solution.py:597
  4.2 1.5 %collective-permute-start.1 = (f32[96,128]{1,0:T(8,128)S(1)}, f32[96,128]{1,0:T(8,128)S(1)}, u32[]{:S(2)}, u32[]{:S(2)}) collective-permute-start(f32[96,128]{1,0:T(8,128)S(1)} %get-tuple-element.22), channel_id=1, source_target_pairs={{0,1},{1,0},{2,4},{3,5},{4,2},{5,3},{6,7},{7,6},{8,9},{9,8},{10,12... | collective-permute-start | bytes 147464 | tf_op jit(solution)/shard_map/ppermute | solution.py:598
  5.7 0.0 copy-done.3
  5.7 0.0 copy-done.4
  5.7 0.0 copy-done.5
  5.7 0.0 copy-done.6
  5.7 0.0 copy-done.7
  5.7 0.0 copy-done.10
  5.7 0.0 copy-done.11
  5.7 0.0 copy-done.12
  5.7 0.0 copy-done.8
  5.7 0.0 copy-done.9
  5.8 0.0 copy-start.2
  5.8 1.0 %copy-done.2 = bf16[2,2,256,256]{3,2,1,0:T(8,128)(2,1)S(1)} copy-done((bf16[2,2,256,256]{3,2,1,0:T(8,128)(2,1)S(1)}, bf16[2,2,256,256]{3,2,1,0:T(8,128)(2,1)}, u32[]{:S(2)}) %copy-start.2) | copy-done | bytes 524312
  6.8 1.3 %prepare.1 = (f32[5,2,80,128]{3,2,1,0:T(8,128)S(1)}, f32[80,128]{1,0:T(8,128)S(1)}, f32[80,128]{1,0:T(8,128)S(1)}, f32[80,128]{1,0:T(8,128)S(1)}, f32[2,32,8,128...) custom-call(f32[5,2,64,128]{3,2,1,0:T(8,128)S(1)} %copy-done, ...), custom_call_target="tpu_custom_call" | custom-call | tf_op jit(solution)/shard_map/prepare/pallas_call | solution.py:579
  8.1 0.0 collective-permute-done.first_round
  8.1 0.2 %collective-permute-done.1.second_round = f32[96,128]{1,0:T(8,128)S(1)} collective-permute-done((f32[96,128]{1,0:T(8,128)S(1)}, f32[96,128]{1,0:T(8,128)S(1)}, u32[]{:S(2)}, u32[]{:S(2)}) %collective-permute-start.1) | collective-permute-done | bytes 49184 | tf_op jit(solution)/shard_map/ppermute | solution.py:598
  8.3 0.1 pack_x.1
  8.4 1.6 %collective-permute-start.2 = (f32[96,128]{1,0:T(8,128)S(1)}, f32[96,128]{1,0:T(8,128)S(1)}, u32[]{:S(2)}, u32[]{:S(2)}) collective-permute-start(f32[96,128]{1,0:T(8,128)S(1)} %pack_x.1), channel_id=1, source_target_pairs={{0,1},{1,0},{2,3},{3,2},{4,5},{5,4},{6,7},{7,6},{8,9},{9,8},{10,11... | collective-permute-start | bytes 147464 | tf_op jit(solution)/shard_map/ppermute | solution.py:643
  10.0 0.0 copy-done.1
  10.0 0.8 %begin.1 = (f32[5,2,80,128]{3,2,1,0:T(8,128)S(1)}, f32[5,2,80,128]{3,2,1,0:T(8,128)S(1)}, f32[5,2,80,128]{3,2,1,0:T(8,128)S(1)}, f32[80,128]{1,0:T(8,128)S(1)}) custom-call(f32[5,2,64,128]{3,2,1,0:T(8,128)S(1)} %copy-done.1, f32[96,128]{1,0:T(8,128)S(1)} %collective-permute-done.first_round, f32[96,128]{1,0:T(8,128)S(1)} %collective-permute-done.1.second_round, ...), custom_call_target="tpu_custom_call" | custom-call | tf_op jit(solution)/shard_map/begin/pallas_call | solution.py:579
  10.8 1.8 %collective-permute-done.2.refs_0_ = f32[96,128]{1,0:T(8,128)S(1)} collective-permute-done((f32[96,128]{1,0:T(8,128)S(1)}, f32[96,128]{1,0:T(8,128)S(1)}, u32[]{:S(2)}, u32[]{:S(2)}) %collective-permute-start.2) | collective-permute-done | bytes 49184 | tf_op jit(solution)/shard_map/ppermute | solution.py:643
  12.6 2.9 %finish.1 = f32[5,2,64,128]{3,2,1,0:T(8,128)} custom-call(f32[96,128]{1,0:T(8,128)S(1)} %collective-permute-done.2.refs_0_, f32[80,128]{1,0:T(8,128)S(1)} %get-tuple-element.28.refs_1_, f32[80,128]{1,0:T(8,128)S(1)} %get-tuple-element.29.refs_2_, bf16[256,256]{1,0:T(8,128)(2,1)S(1)} %get-tuple-element.30.refs_3_, ...), custom_call_target="tpu_custom_call" | custom-call | tf_op jit(solution)/shard_map/finish/pallas_call | solution.py:579
  (5 shorter events, 0.0 us)
Async XLA Ops:
  0.0 1.0 %copy-start = (f32[5,2,64,128]{3,2,1,0:T(8,128)S(1)}, f32[5,2,64,128]{3,2,1,0:T(8,128)}, u32[]{:S(2)}) copy-start(f32[5,2,64,128]{3,2,1,0:T(8,128)} %fields.5) | copy-start | bytes 983044
  1.0 4.7 %copy-start.3 = (bf16[2,128,128]{2,1,0:T(8,128)(2,1)S(1)}, bf16[2,128,128]{2,1,0:T(8,128)(2,1)}, u32[]{:S(2)}) copy-start(bf16[2,128,128]{2,1,0:T(8,128)(2,1)} %constant.4.clone.own_band) | copy-start | bytes 196612
  1.0 4.7 %copy-start.4 = (bf16[5,2,8,256]{3,2,1,0:T(8,128)(2,1)S(1)}, bf16[5,2,8,256]{3,2,1,0:T(8,128)(2,1)}, u32[]{:S(2)}) copy-start(bf16[5,2,8,256]{3,2,1,0:T(8,128)(2,1)} %north.1) | copy-start | bytes 122884
  1.0 4.7 %copy-start.5 = (bf16[5,2,8,256]{3,2,1,0:T(8,128)(2,1)S(1)}, bf16[5,2,8,256]{3,2,1,0:T(8,128)(2,1)}, u32[]{:S(2)}) copy-start(bf16[5,2,8,256]{3,2,1,0:T(8,128)(2,1)} %south.1) | copy-start | bytes 122884
  1.0 4.7 %copy-start.6 = (bf16[5,2,256,8]{2,3,1,0:T(8,128)(2,1)S(1)}, bf16[5,2,256,8]{2,3,1,0:T(8,128)(2,1)}, u32[]{:S(2)}) copy-start(bf16[5,2,256,8]{2,3,1,0:T(8,128)(2,1)} %param.18) | copy-start | bytes 122884
  1.0 4.7 %copy-start.7 = (bf16[5,2,256,8]{2,3,1,0:T(8,128)(2,1)S(1)}, bf16[5,2,256,8]{2,3,1,0:T(8,128)(2,1)}, u32[]{:S(2)}) copy-start(bf16[5,2,256,8]{2,3,1,0:T(8,128)(2,1)} %param.19) | copy-start | bytes 122884
  1.0 4.7 %copy-start.10 = (s32[4]{0:T(128)S(1)}, s32[4]{0:T(128)}, u32[]{:S(2)}) copy-start(s32[4]{0:T(128)} %widths.1) | copy-start | bytes 52
  1.0 4.7 %copy-start.11 = (f32[2]{0:T(128)S(1)}, f32[2]{0:T(128)}, u32[]{:S(2)}) copy-start(f32[2]{0:T(128)} %wind_x.1) | copy-start | bytes 28
  1.0 4.7 %copy-start.12 = (f32[2]{0:T(128)S(1)}, f32[2]{0:T(128)}, u32[]{:S(2)}) copy-start(f32[2]{0:T(128)} %wind_y.1) | copy-start | bytes 28
  1.1 4.7 %copy-start.8 = (f32[2,5,5]{2,0,1:T(2,128)S(1)}, f32[2,5,5]{2,0,1:T(2,128)}, u32[]{:S(2)}) copy-start(f32[2,5,5]{2,0,1:T(2,128)} %param.15) | copy-start | bytes 604
  1.1 7.0 %collective-permute-start = (f32[96,128]{1,0:T(8,128)S(1)}, f32[96,128]{1,0:T(8,128)S(1)}, u32[]{:S(2)}, u32[]{:S(2)}) collective-permute-start(f32[96,128]{1,0:T(8,128)S(1)} %get-tuple-element.21), channel_id=1, source_target_pairs={{0,2},{1,3},{2,0},{3,1},{4,6},{5,7},{6,4},{7,5},{8,10},{9,11},{10,... | collective-permute-start | bytes 147464 | tf_op jit(solution)/shard_map/ppermute | solution.py:597
  4.2 1.6 %copy-start.9 = (f32[4,5,2]{1,2,0:T(2,128)S(1)}, f32[4,5,2]{1,2,0:T(2,128)}, u32[]{:S(2)}) copy-start(f32[4,5,2]{1,2,0:T(2,128)} %param.20) | copy-start | bytes 484
  4.2 4.1 %collective-permute-start.1 = (f32[96,128]{1,0:T(8,128)S(1)}, f32[96,128]{1,0:T(8,128)S(1)}, u32[]{:S(2)}, u32[]{:S(2)}) collective-permute-start(f32[96,128]{1,0:T(8,128)S(1)} %get-tuple-element.22), channel_id=1, source_target_pairs={{0,1},{1,0},{2,4},{3,5},{4,2},{5,3},{6,7},{7,6},{8,9},{9,8},{10,12... | collective-permute-start | bytes 147464 | tf_op jit(solution)/shard_map/ppermute | solution.py:598
  5.8 1.0 %copy-start.2 = (bf16[2,2,256,256]{3,2,1,0:T(8,128)(2,1)S(1)}, bf16[2,2,256,256]{3,2,1,0:T(8,128)(2,1)}, u32[]{:S(2)}) copy-start(bf16[2,2,256,256]{3,2,1,0:T(8,128)(2,1)} %constant.5.clone.side_band) | copy-start | bytes 1572868
  6.8 3.2 %copy-start.1 = (f32[5,2,64,128]{3,2,1,0:T(8,128)S(1)}, f32[5,2,64,128]{3,2,1,0:T(8,128)}, u32[]{:S(2)}) copy-start(f32[5,2,64,128]{3,2,1,0:T(8,128)} %fields.5) | copy-start | bytes 983044
  8.4 4.2 %collective-permute-start.2 = (f32[96,128]{1,0:T(8,128)S(1)}, f32[96,128]{1,0:T(8,128)S(1)}, u32[]{:S(2)}, u32[]{:S(2)}) collective-permute-start(f32[96,128]{1,0:T(8,128)S(1)} %pack_x.1), channel_id=1, source_target_pairs={{0,1},{1,0},{2,3},{3,2},{4,5},{5,4},{6,7},{7,6},{8,9},{9,8},{10,11... | collective-permute-start | bytes 147464 | tf_op jit(solution)/shard_map/ppermute | solution.py:643
